TPU v7x, 512 devices: a whole 4x4x16 slice. The times are simulated.
512 devices in a mesh: blk: 32 (over x, z_lo), rep: 16 (over z_hi, y, core).
Axes of the slice: x: 4, y: 4, z: 16 (z_hi: 2, z_lo: 8; z = z_hi * 8 + z_lo), core: 2. Of those that a mesh axis runs over, the one named last changes fastest.
Arguments:
- signals: bfloat16 [32768, 8192], P('rep', 'blk'), may hold values from -6 to 6
- omega: float32 [32, 5, 256, 256], P('blk', None, 'rep'), may hold values from -1.2 to 3, as said below
- pattern: int32 [32, 5], P('blk'), may hold values from 0 to 31, as said below
Outputs:
- omega_next: float32 [32, 5, 256, 256], P('blk', None, 'rep')
Inputs may be any that keep to these rules, and one draw needn't show every extreme that they name: pattern[i, 0] = i. For two distinct whole numbers A and B from 1 to 15, the same in every row, pattern[i, 1] to pattern[i, 4] are i + A, i - A, i + B and i - B modulo 32 in some order, the same order in every row. Omega is symmetric: omega[i, k] is the transpose of omega[pattern[i, k], k2] where pattern[pattern[i, k], k2] = i. The diagonal entries of omega[i, 0] lie between 1 and 3.
All inputs are finite; a program needn't handle non-finite values.
Results may differ from a plain program's by a relative error of at most 0.0033.
Values may be sent and summed in bfloat16 or wider, within the bound.
A program may use at most 128 MiB of HBM per device.

v0:
```python
import jax
import jax.numpy as jnp
from jax import lax
from jax.sharding import PartitionSpec as P

STEP_SIZE = 0.5
PENALTY = 0.1


def shifted_2(block, axis, distance):
    devices = range(lax.axis_size(axis))
    route = [((i - distance) % len(devices), i) for i in devices]
    return lax.ppermute(block, axis, route)


def advance(stacked, shifted, distance, section_index):
    chosen = jnp.mod(distance // (1 << section_index), 2) == 1
    return jnp.where(chosen[:, None, None], shifted, stacked)


def slot_order(drawn_offsets, team_count):
    slot_ids = jnp.arange(drawn_offsets.shape[0], dtype=jnp.int32)
    partner = jnp.argmax(drawn_offsets == team_count - drawn_offsets[1])
    third = jnp.where(partner == 2, 3, 2).astype(jnp.int32)
    fourth = jnp.where(partner == 4, 3, 4).astype(jnp.int32)
    order = jnp.stack([jnp.zeros((), jnp.int32), jnp.ones((), jnp.int32), partner, third, fourth])
    inverse = jnp.argmax(order[None, :] == slot_ids[:, None], axis=1)
    return (order, inverse)


def per_device(signals, omega, pattern):
    team_count = lax.axis_size("blk")
    replica_count = lax.axis_size("rep")
    level_count = team_count.bit_length() - 1
    team_index = lax.axis_index("blk")
    replica_index = lax.axis_index("rep")
    slot_count = omega.shape[1]
    tile_rows = omega.shape[2]
    tile_width = omega.shape[3]
    time_length = signals.shape[0] * replica_count
    drawn_offsets = jnp.mod(pattern[0] - team_index, team_count)
    order, inverse = slot_order(drawn_offsets, team_count)
    offsets = drawn_offsets[order]
    own_tiles = omega[0][order]
    panels = lax.all_gather(omega.astype(jnp.bfloat16), "rep", axis=2, tiled=True)[0][order]
    remote = jnp.broadcast_to(signals[None], (slot_count - 1,) + signals.shape)
    distance = offsets[1:]
    for section_index in range(level_count):
        shifted = shifted_2(remote, "blk", -(1 << section_index))
        remote = advance(remote, shifted, distance, section_index)
    gathered = jnp.concatenate([signals[None], remote], axis=0)
    mixed = jnp.einsum("ktc,kdc->td", gathered, panels, preferred_element_type=jnp.float32).astype(
        jnp.bfloat16
    )
    left_terms = jnp.einsum("td,ktc->kdc", mixed, gathered, preferred_element_type=jnp.float32)
    stacked = jnp.concatenate([left_terms, jnp.swapaxes(left_terms, 1, 2)], axis=0)
    first_row = replica_index * tile_rows
    summed = lax.psum(stacked, "rep")
    summed = lax.dynamic_slice_in_dim(summed, first_row, tile_rows, 1)
    own_terms = summed[:slot_count]
    flipped = summed[slot_count:]
    mirrored = [
        flipped[slot_index + 1] if slot_index % 2 == 1 else flipped[slot_index - 1]
        for slot_index in range(1, slot_count)
    ]
    outgoing = jnp.stack(mirrored)
    distance = offsets[1:]
    for section_index in range(level_count):
        shifted = shifted_2(outgoing, "blk", -(1 << section_index))
        outgoing = advance(outgoing, shifted, distance, section_index)
    returned = jnp.concatenate([flipped[0:1], outgoing], axis=0)
    gradient = (own_terms + returned) / (2.0 * time_length)
    column_ids = jnp.arange(tile_width, dtype=jnp.int32)
    row_ids = first_row + jnp.arange(tile_rows, dtype=jnp.int32)
    diagonal_mask = column_ids[None, :] == row_ids[:, None]
    diag_values = jnp.sum(jnp.where(diagonal_mask, own_tiles[0], 0.0), axis=1)
    first_grad = gradient[0] - jnp.where(diagonal_mask, (1.0 / diag_values)[:, None], 0.0)
    gradient = jnp.concatenate([first_grad[None], gradient[1:]], axis=0)
    updated = own_tiles - STEP_SIZE * gradient
    shrunk = jnp.sign(updated) * jnp.maximum(jnp.abs(updated) - STEP_SIZE * PENALTY, 0.0)
    slot_ids = jnp.arange(slot_count, dtype=jnp.int32)
    keep_mask = (slot_ids[:, None, None] == 0) & diagonal_mask[None]
    result = jnp.where(keep_mask, updated, shrunk)
    return result[inverse][None]


def solution(mesh):
    return jax.shard_map(
        per_device,
        mesh=mesh,
        in_specs=(P("rep", "blk"), P("blk", None, "rep", None), P("blk", None)),
        out_specs=P("blk", None, "rep", None),
        check_vma=False,
    )
```

profile of v0, /device:TPU:230, one launch (start us, length us, event | category | flops | bytes accessed | tf_op | source)
XLA Modules:
  0.0 1216.6 jit_solution(44980131006456918)
XLA Ops:
  6.5 3.5 broadcast_in_dim.114
  10.1 2.0 collective-permute-start
  16.6 96.7 %collective-permute-done = bf16[4,2048,256]{2,1,0:T(8,128)(2,1)} collective-permute-done((bf16[4,2048,256]{2,1,0:T(8,128)(2,1)}, bf16[4,2048,256]{2,1,0:T(8,128)(2,1)}, u32[]{:S(2)}, u32[]{:S(2)}) %collective-permute-start) | collective-permute-done | bytes 4194336 | tf_op jit(solution)/shard_map/ppermute | solution.py:13
  113.3 2.8 broadcast_select_fusion
  116.1 1.9 collective-permute-start.1
  118.0 180.3 %collective-permute-done.1 = bf16[4,2048,256]{2,1,0:T(8,128)(2,1)S(1)} collective-permute-done((bf16[4,2048,256]{2,1,0:T(8,128)(2,1)S(1)}, bf16[4,2048,256]{2,1,0:T(8,128)(2,1)S(1)}, u32[]{:S(2)}, u32[]{:S(2)}) %collective-permute-start.1) | collective-permute-done | bytes 4194336 | tf_op jit(solution)/shard_map/ppermute | solution.py:13
  298.3 2.8 broadcast_select_fusion.1
  301.1 1.9 collective-permute-start.2
  303.0 356.7 %collective-permute-done.2 = bf16[4,2048,256]{2,1,0:T(8,128)(2,1)S(1)} collective-permute-done((bf16[4,2048,256]{2,1,0:T(8,128)(2,1)S(1)}, bf16[4,2048,256]{2,1,0:T(8,128)(2,1)S(1)}, u32[]{:S(2)}, u32[]{:S(2)}) %collective-permute-start.2) | collective-permute-done | bytes 4194336 | tf_op jit(solution)/shard_map/ppermute | solution.py:13
  660.3 1.9 collective-permute-start.3
  662.2 93.7 %collective-permute-done.3 = bf16[4,2048,256]{2,1,0:T(8,128)(2,1)S(1)} collective-permute-done((bf16[4,2048,256]{2,1,0:T(8,128)(2,1)S(1)}, bf16[4,2048,256]{2,1,0:T(8,128)(2,1)S(1)}, u32[]{:S(2)}, u32[]{:S(2)}) %collective-permute-start.3) | collective-permute-done | bytes 4194336 | tf_op jit(solution)/shard_map/ppermute | solution.py:13
  755.9 2.4 broadcast_select_fusion.3
  760.2 45.1 %all_gather.3 = bf16[1,5,256,256]{3,2,1,0:T(8,128)(2,1)S(1)} all-gather(bf16[1,5,16,256]{3,2,1,0:T(8,128)(2,1)S(1)} %convert_element_type.6), channel_id=1, replica_groups=mesh['blk'=32,'rep'=16] {'rep'}, dimensions={2}, use_global_device_ids=true | all-gather | bytes 696320 | tf_op jit(solution)/shard_map/all_gather | solution.py:45
  805.9 47.7 %collective-permute-done.4 = bf16[4,2048,256]{2,1,0:T(8,128)(2,1)} collective-permute-done((bf16[4,2048,256]{2,1,0:T(8,128)(2,1)}, bf16[4,2048,256]{2,1,0:T(8,128)(2,1)}, u32[]{:S(2)}, u32[]{:S(2)}) %collective-permute-start.4) | collective-permute-done | bytes 4194336 | tf_op jit(solution)/shard_map/ppermute | solution.py:13
  853.7 4.0 broadcast_select_fusion.4
  862.5 3.0 pad_maximum_fusion.5
  867.4 282.8 %all-reduce.2.cloned.1.call-done = f32[10,256,256]{2,1,0:T(8,128)} async-done(((f32[10,256,256]{2,1,0:T(8,128)}), f32[10,256,256]{2,1,0:T(8,128)}) %all-reduce.2.cloned.1.call-update) | async-done | bytes 2621456 | tf_op jit(solution)/shard_map/psum | solution.py:58
  1151.0 2.0 collective-permute-start.5
  1153.2 12.7 %collective-permute-done.5 = f32[4,16,256]{2,1,0:T(8,128)S(1)} collective-permute-done((f32[4,16,256]{2,1,0:T(8,128)S(1)}, f32[4,16,256]{2,1,0:T(8,128)S(1)}, u32[]{:S(2)}, u32[]{:S(2)}) %collective-permute-start.5) | collective-permute-done | bytes 65568 | tf_op jit(solution)/shard_map/ppermute | solution.py:13
  1167.9 12.1 collective-permute-done.6
  1180.1 1.9 collective-permute-start.7
  1182.1 10.2 collective-permute-done.7
  1194.3 5.4 collective-permute-done.8
  1201.7 5.7 collective-permute-done.9
  (48 shorter events, 21.8 us)
Async XLA Ops:
  6.5 106.8 %copy-start = (bf16[2048,256]{1,0:T(8,128)(2,1)S(1)}, bf16[2048,256]{1,0:T(8,128)(2,1)}, u32[]{:S(2)}) copy-start(bf16[2048,256]{1,0:T(8,128)(2,1)} %param.3) | copy-start | bytes 3145732
  6.5 5.5 copy-start.2
  6.5 1143.7 %all-reduce.2.cloned.1.call-start = ((), (), s32[]{:S(2)}) async-start(), calls=%async_computation | async-start | bytes 5242880 | tf_op jit(solution)/shard_map/psum | solution.py:58
  10.1 103.2 %collective-permute-start = (bf16[4,2048,256]{2,1,0:T(8,128)(2,1)}, bf16[4,2048,256]{2,1,0:T(8,128)(2,1)}, u32[]{:S(2)}, u32[]{:S(2)}) collective-permute-start(bf16[4,2048,256]{2,1,0:T(8,128)(2,1)} %broadcast_in_dim.114), channel_id=1, source_target_pairs={{16,0},{32,16},{48,32},{64,48},{80,64},{96,80},{112,96},{128,112},... | collective-permute-start | bytes 12582920 | tf_op jit(solution)/shard_map/ppermute | solution.py:13
  116.1 182.3 %collective-permute-start.1 = (bf16[4,2048,256]{2,1,0:T(8,128)(2,1)S(1)}, bf16[4,2048,256]{2,1,0:T(8,128)(2,1)S(1)}, u32[]{:S(2)}, u32[]{:S(2)}) collective-permute-start(bf16[4,2048,256]{2,1,0:T(8,128)(2,1)S(1)} %broadcast_select_fusion), channel_id=1, source_target_pairs={{32,0},{48,16},{64,32},{80,48},{96,64},{112,80},{128,96},{144,112}... | collective-permute-start | bytes 12582920 | tf_op jit(solution)/shard_map/ppermute | solution.py:13
  301.1 358.7 %collective-permute-start.2 = (bf16[4,2048,256]{2,1,0:T(8,128)(2,1)S(1)}, bf16[4,2048,256]{2,1,0:T(8,128)(2,1)S(1)}, u32[]{:S(2)}, u32[]{:S(2)}) collective-permute-start(bf16[4,2048,256]{2,1,0:T(8,128)(2,1)S(1)} %broadcast_select_fusion.1), channel_id=1, source_target_pairs={{64,0},{80,16},{96,32},{112,48},{128,64},{144,80},{160,96},{176,11... | collective-permute-start | bytes 12582920 | tf_op jit(solution)/shard_map/ppermute | solution.py:13
  660.3 95.6 %collective-permute-start.3 = (bf16[4,2048,256]{2,1,0:T(8,128)(2,1)S(1)}, bf16[4,2048,256]{2,1,0:T(8,128)(2,1)S(1)}, u32[]{:S(2)}, u32[]{:S(2)}) collective-permute-start(bf16[4,2048,256]{2,1,0:T(8,128)(2,1)S(1)} %broadcast_select_fusion.2), channel_id=1, source_target_pairs={{128,0},{144,16},{160,32},{176,48},{192,64},{208,80},{224,96},{240... | collective-permute-start | bytes 12582920 | tf_op jit(solution)/shard_map/ppermute | solution.py:13
  755.9 4.3 copy-start.1
  758.3 95.4 %collective-permute-start.4 = (bf16[4,2048,256]{2,1,0:T(8,128)(2,1)}, bf16[4,2048,256]{2,1,0:T(8,128)(2,1)}, u32[]{:S(2)}, u32[]{:S(2)}) collective-permute-start(bf16[4,2048,256]{2,1,0:T(8,128)(2,1)} %broadcast_select_fusion.3), channel_id=1, source_target_pairs={{256,0},{272,16},{288,32},{304,48},{320,64},{336,80},{352,96},{368... | collective-permute-start | bytes 12582920 | tf_op jit(solution)/shard_map/ppermute | solution.py:13
  1151.0 14.9 %collective-permute-start.5 = (f32[4,16,256]{2,1,0:T(8,128)S(1)}, f32[4,16,256]{2,1,0:T(8,128)S(1)}, u32[]{:S(2)}, u32[]{:S(2)}) collective-permute-start(f32[4,16,256]{2,1,0:T(8,128)S(1)} %pad_maximum_fusion.10), channel_id=1, source_target_pairs={{16,0},{32,16},{48,32},{64,48},{80,64},{96,80},{112,96},{128,112},... | collective-permute-start | bytes 196616 | tf_op jit(solution)/shard_map/ppermute | solution.py:13
  1166.0 14.1 %collective-permute-start.6 = (f32[4,16,256]{2,1,0:T(8,128)S(1)}, f32[4,16,256]{2,1,0:T(8,128)S(1)}, u32[]{:S(2)}, u32[]{:S(2)}) collective-permute-start(f32[4,16,256]{2,1,0:T(8,128)S(1)} %broadcast_select_fusion.5), channel_id=1, source_target_pairs={{32,0},{48,16},{64,32},{80,48},{96,64},{112,80},{128,96},{144,112}... | collective-permute-start | bytes 196616 | tf_op jit(solution)/shard_map/ppermute | solution.py:13
  1180.1 12.2 %collective-permute-start.7 = (f32[4,16,256]{2,1,0:T(8,128)S(1)}, f32[4,16,256]{2,1,0:T(8,128)S(1)}, u32[]{:S(2)}, u32[]{:S(2)}) collective-permute-start(f32[4,16,256]{2,1,0:T(8,128)S(1)} %broadcast_select_fusion.6), channel_id=1, source_target_pairs={{64,0},{80,16},{96,32},{112,48},{128,64},{144,80},{160,96},{176,11... | collective-permute-start | bytes 196616 | tf_op jit(solution)/shard_map/ppermute | solution.py:13
  1192.4 7.4 collective-permute-start.8
  1199.8 7.7 collective-permute-start.9
Sparse Core Ops, SparseCore 0:
  865.6 284.5 all-reduce.1
where the time goes:
time: 1220 us
  waiting for transfers between devices  1100 us (90%)
  blocking collectives  45.1 us (4%)
  starting transfers between devices  19.3 us (2%)
  other arithmetic  18.6 us (2%)
  between operations  15.4 us (1%)
    ppermute x10, waiting for transfers between devices, shifted_2(): return lax.ppermute(block, axis, route)  821 us
    psum x1, waiting for transfers between devices, per_device(): summed = lax.psum(stacked, 'rep')  283 us
    all_gather x1, blocking collectives, per_device(): lax.all_gather(omega.astype(jnp.bfloat16), 'rep', axis=2, tiled=True)[0]  45.1 us
  transfers between devices with their start and end apart: 11, of which 11 were waited for; matrix products, arithmetic and copies ran while one was open for 0% of the time, Pallas kernels for 0%

commit v1 on v0

v1 whole, which is shorter than its diff:
```python
import jax
import jax.numpy as jnp
from jax import lax
from jax.sharding import Mesh
from jax.sharding import PartitionSpec as P

STEP_SIZE = 0.5
PENALTY = 0.1
REP = ("zh", "y", "c")


def fine_mesh(mesh):
    return Mesh(mesh.devices.reshape(4, 8, 2, 4, 2), ("x", "zl", "zh", "y", "c"))


def per_device(signals, omega, pattern):
    x_size = lax.axis_size("x")
    zl_size = lax.axis_size("zl")
    team_count = x_size * zl_size
    replica_count = lax.axis_size(REP)
    team_index = lax.axis_index(("x", "zl"))
    replica_index = lax.axis_index(REP)
    slot_count, tile_rows, width = omega.shape[1:]
    time_length = signals.shape[0] * replica_count
    offsets = jnp.mod(pattern[0] - team_index, team_count)

    own = signals.reshape(zl_size, signals.shape[0] // zl_size, width)
    blocks = lax.all_to_all(own, "zl", 0, 0, tiled=True)
    blocks = lax.all_gather(blocks, "x", axis=0, tiled=True)
    panels = lax.all_gather(omega.astype(jnp.bfloat16), REP, axis=2, tiled=True)
    panels = lax.all_gather(panels, "zl", axis=0, tiled=True)

    rows = lax.axis_index("x") * zl_size + jnp.arange(zl_size, dtype=jnp.int32)
    columns = jnp.mod(rows[:, None] + offsets[None, :], team_count)
    gathered = blocks[columns]
    mixed = jnp.einsum("jktc,jkdc->jtd", gathered, panels, preferred_element_type=jnp.float32).astype(jnp.bfloat16)
    left = jnp.einsum("jtd,jktc->jkdc", mixed, gathered, preferred_element_type=jnp.float32)

    own_terms = lax.psum_scatter(left, REP, scatter_dimension=2, tiled=True)
    own_terms = lax.psum_scatter(own_terms, "zl", scatter_dimension=0, tiled=True)[0]
    flipped = lax.all_to_all(own_terms, REP, 2, 1, tiled=True)
    flipped = jnp.swapaxes(flipped, 1, 2)
    match = offsets[None, :] == jnp.mod(team_count - offsets, team_count)[:, None]
    mirror = jnp.argmax(match, axis=1)
    outgoing = flipped[mirror]
    for level in range(team_count.bit_length() - 1):
        step = 1 << level
        route = [((i + step) % team_count, i) for i in range(team_count)]
        shifted = lax.ppermute(outgoing, ("x", "zl"), route)
        chosen = jnp.mod(offsets // step, 2) == 1
        outgoing = jnp.where(chosen[:, None, None], shifted, outgoing)

    gradient = (own_terms + outgoing) / (2.0 * time_length)
    tiles = omega[0]
    column_ids = jnp.arange(width, dtype=jnp.int32)
    row_ids = replica_index * tile_rows + jnp.arange(tile_rows, dtype=jnp.int32)
    diagonal = column_ids[None, :] == row_ids[:, None]
    diagonal = diagonal[None] & (offsets == 0)[:, None, None]
    gradient = gradient - jnp.where(diagonal, 1.0 / jnp.where(diagonal, tiles, 1.0), 0.0)
    value = tiles - STEP_SIZE * gradient
    shrunk = jnp.sign(value) * jnp.maximum(jnp.abs(value) - STEP_SIZE * PENALTY, 0.0)
    return jnp.where(diagonal, value, shrunk)[None]


def solution(mesh):
    return jax.shard_map(
        per_device,
        mesh=fine_mesh(mesh),
        in_specs=(P(REP, ("x", "zl")), P(("x", "zl"), None, REP, None), P(("x", "zl"), None)),
        out_specs=P(("x", "zl"), None, REP, None),
        check_vma=False,
    )
```

time: 1220 us -> 670 us (0.55)
  waiting for transfers between devices: 1100 us -> 490 us
  blocking collectives: 45.1 us -> 101 us
  local copies, waits for them, and re-layouts: 10.7 us -> 25 us
  other arithmetic: 18.6 us -> 4.41 us
    ppermute x10 -> x5, waiting for transfers between devices: 821 us -> 47.2 us  [per_device(): shifted = lax.ppermute(outgoing, ('x', 'zl'), route)]
    reduce_scatter x0 -> x2, waiting for transfers between devices: none -> 303 us  [the longest x1 245 us: per_device(): own_terms = lax.psum_scatter(left, REP, scatter_dimension=2, tiled=True)]
    psum x1 -> x0, waiting for transfers between devices: 283 us -> none  [per_device(): summed = lax.psum(stacked, 'rep')]
    all_gather x0 -> x2, waiting for transfers between devices: none -> 124 us  [the longest x1 114 us: per_device(): panels = lax.all_gather(panels, 'zl', axis=0, tiled=True)]
    all_to_all x0 -> x1, blocking collectives: none -> 55.6 us  [per_device(): blocks = lax.all_to_all(own, 'zl', 0, 0, tiled=True)]
    all_to_all x0 -> x1, waiting for transfers between devices: none -> 15 us  [per_device(): flipped = lax.all_to_all(own_terms, REP, 2, 1, tiled=True)]
    all_to_all x0 -> x1, starting transfers between devices: none -> 14.2 us  [per_device(): flipped = lax.all_to_all(own_terms, REP, 2, 1, tiled=True)]
    select_n x14 -> x7, other arithmetic: 12.9 us -> 0.4 us  [the longest x4 0.3 us: per_device(): outgoing = jnp.where(chosen[:, None, None], shifted, outgoing)]
  transfers between devices with their start and end apart: 11 -> 10, of which waited for: 11 -> 10; matrix products, arithmetic and copies ran while one was open for 0% -> 1% of each run, Pallas kernels for 0% -> 0%
where the time goes in v1:
time: 670 us; the launch traced here: 669 us
  waiting for transfers between devices  490 us (73%)
  blocking collectives  101 us (15%)
  local copies, waits for them, and re-layouts  25 us (4%)
  starting transfers between devices  23.9 us (4%)
  between operations  13.3 us (2%)
  matrix products  12.5 us (2%)
    reduce_scatter x1, waiting for transfers between devices, per_device(): own_terms = lax.psum_scatter(left, REP, scatter_dimension=2, tiled=True)  245 us
    all_gather x1, waiting for transfers between devices, per_device(): panels = lax.all_gather(panels, 'zl', axis=0, tiled=True)  114 us
    reduce_scatter x1, waiting for transfers between devices, per_device(): lax.psum_scatter(own_terms, 'zl', scatter_dimension=0, tiled=True)[0]  58.2 us
    all_to_all x1, blocking collectives, per_device(): blocks = lax.all_to_all(own, 'zl', 0, 0, tiled=True)  55.6 us
    ppermute x5, waiting for transfers between devices, per_device(): shifted = lax.ppermute(outgoing, ('x', 'zl'), route)  47.2 us
    all_gather x1, blocking collectives, per_device(): panels = lax.all_gather(omega.astype(jnp.bfloat16), REP, axis=2, tiled=True)  45.3 us
    all_to_all x1, waiting for transfers between devices, per_device(): flipped = lax.all_to_all(own_terms, REP, 2, 1, tiled=True)  15 us
    all_to_all x1, starting transfers between devices, per_device(): flipped = lax.all_to_all(own_terms, REP, 2, 1, tiled=True)  14.2 us
  transfers between devices with their start and end apart: 10, of which 10 were waited for; matrix products, arithmetic and copies ran while one was open for 1% of the time, Pallas kernels for 0%

profile of v1, /device:TPU:230, one launch (start us, length us, event | category | flops | bytes accessed | tf_op | source)
XLA Modules:
  0.0 669.5 jit_solution(8638916152552195182)
XLA Ops:
  6.5 55.6 %all_to_all.23 = bf16[8,256,256]{2,1,0:T(8,128)(2,1)} all-to-all(bf16[8,256,256]{2,1,0:T(8,128)(2,1)} %bitcast.50), channel_id=1, replica_groups=mesh['x'=4,'zl'=8,'zh'=2,'y'=4,'c'=2] {'zl'}, dimensions={0} | all-to-all | bytes 2097152 | tf_op jit(solution)/shard_map/all_to_all | solution.py:28
  63.1 45.3 %all_gather.10 = bf16[1,5,256,256]{3,2,1,0:T(8,128)(2,1)} all-gather(bf16[1,5,16,256]{3,2,1,0:T(8,128)(2,1)S(1)} %convert_element_type.6), channel_id=1, replica_groups=mesh['x'=4,'zl'=8,'zh'=2,'y'=4,'c'=2] {'zh','y','c'}, dimensions={2}, use_global_device_ids=true | all-gather | bytes 696320 | tf_op jit(solution)/shard_map/all_gather | solution.py:30
  109.3 10.0 %all-gather.3.cloned.1.call-done = bf16[32,256,256]{2,1,0:T(8,128)(2,1)} async-done(((bf16[8,256,256]{2,1,0:T(8,128)(2,1)}), bf16[32,256,256]{2,1,0:T(8,128)(2,1)}) %all-gather.3.cloned.1.call-update) | async-done | bytes 4194320 | tf_op jit(solution)/shard_map/all_gather | solution.py:29
  119.3 6.7 %gather_fusion = bf16[40,256,256]{2,1,0:T(8,128)(2,1)} fusion(bf16[32,256,256]{2,1,0:T(8,128)(2,1)} %all-gather.3.cloned.1.call-done, s32[1024]{0:T(1024)S(1)} %pad_clamp_fusion.1), kind=kCustom, calls=%fused_computation | custom fusion | bytes 10485920 | tf_op jit(solution)/shard_map/gather | solution.py:35
  126.0 114.0 %all-gather.5.cloned.1.call-done = bf16[8,5,256,256]{3,2,1,0:T(8,128)(2,1)} async-done(((bf16[1,5,256,256]{3,2,1,0:T(8,128)(2,1)}), bf16[8,5,256,256]{3,2,1,0:T(8,128)(2,1)}) %all-gather.5.cloned.1.call-update) | async-done | bytes 5242896 | tf_op jit(solution)/shard_map/all_gather | solution.py:31
  240.0 12.5 %convolution_bitcast_fusion = f32[8,5,256,256]{2,3,1,0:T(8,128)} fusion(bf16[8,5,256,256]{3,2,1,0:T(8,128)(2,1)} %bitcast.46, bf16[8,5,256,256]{3,2,1,0:T(8,128)(2,1)} %all-gather.5.cloned.1.call-done), kind=kOutput, calls=%fused_computation.2 | convolution fusion | flops 2684878848 | bytes 20971520 | tf_op jit(solution)/shard_map/jtd,jktc->jkdc/dot_general | solution.py:37
  252.5 11.6 %copy.24 = f32[8,5,256,256]{3,0,1,2:T(8,128)} copy(f32[8,5,256,256]{2,3,1,0:T(8,128)} %convolution_bitcast_fusion) | data formatting | bytes 20971520 | tf_op jit(solution)/shard_map/jtd,jktc->jkdc/transpose | solution.py:37
  264.2 245.1 %reduce-scatter.3.cloned.1.call-done = f32[8,5,16,256]{3,0,1,2:T(8,128)} async-done(((f32[8,5,256,256]{3,0,1,2:T(8,128)}), f32[8,5,16,256]{3,0,1,2:T(8,128)}) %reduce-scatter.3.cloned.1.call-update) | async-done | bytes 655376 | tf_op jit(solution)/shard_map/reduce_scatter | solution.py:39
  509.3 2.1 copy.25
  512.2 58.2 %reduce-scatter.5.cloned.1.call-done = f32[1,5,16,256]{3,2,1,0:T(8,128)} async-done(((f32[8,5,16,256]{3,2,1,0:T(8,128)}), f32[1,5,16,256]{3,2,1,0:T(8,128)}) %reduce-scatter.5.cloned.1.call-update) | async-done | bytes 81936 | tf_op jit(solution)/shard_map/reduce_scatter | solution.py:40
  570.4 1.4 copy.26
  571.8 1.0 reshape.312
  572.8 14.2 %all-to-all-start.1 = ((f32[16,1,1280]{2,1,0:T(1,128)}), f32[16,1,1280]{2,1,0:T(1,128)S(1)}, u32[]{:S(2)}, u32[]{:S(2)}) async-start(f32[16,1,1280]{2,1,0:T(1,128)} %reshape.312), calls=%async_computation.3 | async-start | bytes 163840 | tf_op jit(solution)/shard_map/all_to_all | solution.py:41
  587.0 15.0 %all-to-all-done.1 = f32[16,1,1280]{2,1,0:T(1,128)S(1)} async-done(((f32[16,1,1280]{2,1,0:T(1,128)}), f32[16,1,1280]{2,1,0:T(1,128)S(1)}, u32[]{:S(2)}, u32[]{:S(2)}) %all-to-all-start.1) | async-done | bytes 81952 | tf_op jit(solution)/shard_map/all_to_all | solution.py:41
  604.9 1.9 collective-permute-start
  606.9 13.1 %collective-permute-done = f32[5,16,256]{2,1,0:T(8,128)S(1)} collective-permute-done((f32[5,16,256]{2,1,0:T(8,128)S(1)}, f32[5,16,256]{2,1,0:T(8,128)S(1)}, u32[]{:S(2)}, u32[]{:S(2)}) %collective-permute-start) | collective-permute-done | bytes 81952 | tf_op jit(solution)/shard_map/ppermute | solution.py:49
  620.1 1.9 collective-permute-start.1
  622.0 12.3 %collective-permute-done.1 = f32[5,16,256]{2,1,0:T(8,128)S(1)} collective-permute-done((f32[5,16,256]{2,1,0:T(8,128)S(1)}, f32[5,16,256]{2,1,0:T(8,128)S(1)}, u32[]{:S(2)}, u32[]{:S(2)}) %collective-permute-start.1) | collective-permute-done | bytes 81952 | tf_op jit(solution)/shard_map/ppermute | solution.py:49
  634.3 1.9 collective-permute-start.2
  636.2 10.4 %collective-permute-done.2 = f32[5,16,256]{2,1,0:T(8,128)S(1)} collective-permute-done((f32[5,16,256]{2,1,0:T(8,128)S(1)}, f32[5,16,256]{2,1,0:T(8,128)S(1)}, u32[]{:S(2)}, u32[]{:S(2)}) %collective-permute-start.2) | collective-permute-done | bytes 81952 | tf_op jit(solution)/shard_map/ppermute | solution.py:49
  646.7 1.9 collective-permute-start.3
  648.7 5.6 collective-permute-done.3
  654.3 1.9 collective-permute-start.4
  656.3 5.8 collective-permute-done.4
  (39 shorter events, 6.8 us)
Async XLA Ops:
  6.5 112.7 %all-gather.3.cloned.1.call-start = ((), (), s32[]{:S(2)}) async-start(), calls=%async_computation.4 | async-start | bytes 5242880 | tf_op jit(solution)/shard_map/all_gather | solution.py:29
  62.1 177.9 %all-gather.5.cloned.1.call-start = ((), (), s32[]{:S(2)}) async-start(), calls=%async_computation.5 | async-start | bytes 5898240 | tf_op jit(solution)/shard_map/all_gather | solution.py:31
  108.4 400.9 %reduce-scatter.3.cloned.1.call-start = ((), (), s32[]{:S(2)}) async-start(), calls=%async_computation.6 | async-start | bytes 11141120 | tf_op jit(solution)/shard_map/reduce_scatter | solution.py:39
  264.1 247.4 %copy-start.2 = (s32[1,5]{1,0:T(1,128)S(1)}, s32[1,5]{1,0:T(1,128)}, u32[]{:S(2)}) copy-start(s32[1,5]{1,0:T(1,128)} %param.5) | copy-start | bytes 64
  264.2 398.0 %copy-start.1 = (f32[1,5,16,256]{3,2,1,0:T(8,128)S(1)}, f32[1,5,16,256]{3,2,1,0:T(8,128)}, u32[]{:S(2)}) copy-start(f32[1,5,16,256]{3,2,1,0:T(8,128)} %param.4) | copy-start | bytes 245764
  264.2 306.2 %reduce-scatter.5.cloned.1.call-start = ((), (), s32[]{:S(2)}) async-start(), calls=%async_computation.7 | async-start | bytes 737280 | tf_op jit(solution)/shard_map/reduce_scatter | solution.py:40
  570.4 91.8 %copy-start = (f32[1,5,16,256]{3,2,1,0:T(8,128)S(1)}, f32[1,5,16,256]{3,2,1,0:T(8,128)}, u32[]{:S(2)}) copy-start(f32[1,5,16,256]{3,2,1,0:T(8,128)} %reduce-scatter.5.cloned.1.call-done) | copy-start | bytes 245764
  572.8 29.2 %all-to-all-start.1 = ((f32[16,1,1280]{2,1,0:T(1,128)}), f32[16,1,1280]{2,1,0:T(1,128)S(1)}, u32[]{:S(2)}, u32[]{:S(2)}) async-start(f32[16,1,1280]{2,1,0:T(1,128)} %reshape.312), calls=%async_computation.3 | async-start | bytes 163840 | tf_op jit(solution)/shard_map/all_to_all | solution.py:41
  604.9 15.0 %collective-permute-start = (f32[5,16,256]{2,1,0:T(8,128)S(1)}, f32[5,16,256]{2,1,0:T(8,128)S(1)}, u32[]{:S(2)}, u32[]{:S(2)}) collective-permute-start(f32[5,16,256]{2,1,0:T(8,128)S(1)} %gather_fusion.1), channel_id=1, source_target_pairs={{16,0},{32,16},{48,32},{64,48},{80,64},{96,80},{112,96},{128,112},... | collective-permute-start | bytes 245768 | tf_op jit(solution)/shard_map/ppermute | solution.py:49
  620.1 14.2 %collective-permute-start.1 = (f32[5,16,256]{2,1,0:T(8,128)S(1)}, f32[5,16,256]{2,1,0:T(8,128)S(1)}, u32[]{:S(2)}, u32[]{:S(2)}) collective-permute-start(f32[5,16,256]{2,1,0:T(8,128)S(1)} %broadcast_select_fusion), channel_id=1, source_target_pairs={{32,0},{48,16},{64,32},{80,48},{96,64},{112,80},{128,96},{144,112}... | collective-permute-start | bytes 245768 | tf_op jit(solution)/shard_map/ppermute | solution.py:49
  634.3 12.3 %collective-permute-start.2 = (f32[5,16,256]{2,1,0:T(8,128)S(1)}, f32[5,16,256]{2,1,0:T(8,128)S(1)}, u32[]{:S(2)}, u32[]{:S(2)}) collective-permute-start(f32[5,16,256]{2,1,0:T(8,128)S(1)} %broadcast_select_fusion.1), channel_id=1, source_target_pairs={{64,0},{80,16},{96,32},{112,48},{128,64},{144,80},{160,96},{176,11... | collective-permute-start | bytes 245768 | tf_op jit(solution)/shard_map/ppermute | solution.py:49
  646.7 7.5 %collective-permute-start.3 = (f32[5,16,256]{2,1,0:T(8,128)S(1)}, f32[5,16,256]{2,1,0:T(8,128)S(1)}, u32[]{:S(2)}, u32[]{:S(2)}) collective-permute-start(f32[5,16,256]{2,1,0:T(8,128)S(1)} %broadcast_select_fusion.2), channel_id=1, source_target_pairs={{128,0},{144,16},{160,32},{176,48},{192,64},{208,80},{224,96},{240... | collective-permute-start | bytes 245768 | tf_op jit(solution)/shard_map/ppermute | solution.py:49
  654.3 7.8 %collective-permute-start.4 = (f32[5,16,256]{2,1,0:T(8,128)S(1)}, f32[5,16,256]{2,1,0:T(8,128)S(1)}, u32[]{:S(2)}, u32[]{:S(2)}) collective-permute-start(f32[5,16,256]{2,1,0:T(8,128)S(1)} %broadcast_select_fusion.3), channel_id=1, source_target_pairs={{256,0},{272,16},{288,32},{304,48},{320,64},{336,80},{352,96},{368... | collective-permute-start | bytes 245768 | tf_op jit(solution)/shard_map/ppermute | solution.py:49
Sparse Core Ops, SparseCore 0:
  62.2 56.9 all-gather.2
  121.4 118.6 all-gather.4
  264.3 245.0 reduce-scatter.2
  512.3 58.1 reduce-scatter.4

commit v2 on v1

v2 whole, which is shorter than its diff:
```python
import jax
import jax.numpy as jnp
from jax import lax
from jax.experimental import pallas as pl
from jax.experimental.pallas import tpu as pltpu
from jax.sharding import Mesh
from jax.sharding import PartitionSpec as P

STEP_SIZE = 0.5
PENALTY = 0.1
REP = ("zh", "y", "c")
MESH = pl.DeviceIdType.MESH
NX, NZ, NH, NY, NC = 4, 8, 2, 4, 2
Z_ORDER = (4, 5, 6, 7, 1, 2, 3)


def fine_mesh(mesh):
    return Mesh(mesh.devices.reshape(NX, NZ, NH, NY, NC), ("x", "zl", "zh", "y", "c"))


def flip(value, bits):
    for level in range(3):
        weight = 1 << level
        if bits & weight:
            value = value + weight * (1 - 2 * ((value // weight) % 2))
    return value


def remote(src, dst, send, recv, where):
    return pltpu.make_async_remote_copy(
        src_ref=src, dst_ref=dst, send_sem=send, recv_sem=recv, device_id=where, device_id_type=MESH
    )


def exchange_kernel(
    sig, wsh, xout, wout, local_sem, zs, zr, xs_sem, xr, rs, bs, br, ws, wr, ys, yr, cs, cr
):
    x, zl, zh = lax.axis_index("x"), lax.axis_index("zl"), lax.axis_index("zh")
    y, c = lax.axis_index("y"), lax.axis_index("c")
    right, left = {"x": (x + 1) % NX}, {"x": (x + NX - 1) % NX}
    sibling = {"c": 1 - c}
    place = zh * NZ + zl
    ring = NH * NZ
    up, down = (place + 1) % ring, (place + ring - 1) % ring
    up_id = {"zh": up // NZ, "zl": up % NZ}
    down_id = {"zh": down // NZ, "zl": down % NZ}

    barrier = pltpu.get_barrier_semaphore()
    peers = [{"zl": flip(zl, s)} for s in range(1, NZ)] + [right, left, sibling, up_id, down_id]
    peers += [{"y": (y + d) % NY} for d in range(1, NY)]
    for peer in peers:
        pl.semaphore_signal(barrier, inc=1, device_id=peer, device_id_type=MESH)
    pl.semaphore_wait(barrier, len(peers))

    base = c * (NX * NZ)
    mine = base + x * NZ + zl
    own = pltpu.make_async_copy(sig.at[zl], xout.at[mine], local_sem.at[0])
    own.start()
    own_w = pltpu.make_async_copy(wsh, wout.at[c, y, zl, zh], local_sem.at[1])
    own_w.start()
    z_copies = {}
    for s in Z_ORDER:
        peer = flip(zl, s)
        copy = remote(sig.at[peer], xout.at[mine], zs.at[s - 1], zr.at[s - 1], {"zl": peer})
        copy.start()
        z_copies[s] = copy

    def block(dx, s):
        return base + ((x + dx) % NX) * NZ + flip(zl, s)

    def to_sibling(index):
        remote(xout.at[index], xout.at[index], bs, br, sibling).start()

    x_copies = {}

    def spread(s):
        here = xout.at[block(0, s)]
        pair = (
            remote(here, here, xs_sem.at[0, s], xr.at[0, s], right),
            remote(here, here, xs_sem.at[1, s], xr.at[1, s], left),
        )
        for copy in pair:
            copy.start()
        to_sibling(block(0, s))
        x_copies[s] = pair

    relay_copies = {}
    half = xout.shape[1] // 2

    def relay(s):
        pair = []
        for way, (dx, start, where) in enumerate(((NX - 1, 0, right), (1, half, left))):
            x_copies[s][way].wait_recv()
            part = xout.at[block(dx, s), pl.ds(start, half)]
            copy = remote(part, part, rs.at[0, way, s], rs.at[1, way, s], where)
            copy.start()
            to_sibling(block(dx, s))
            pair.append(copy)
        relay_copies[s] = pair

    def finish(s):
        for copy in relay_copies[s]:
            copy.wait_recv()
        to_sibling(block(2, s))

    def shard(origin):
        return wout.at[c, y, origin % NZ, origin // NZ]

    w_copies = []

    def w_step(t):
        if t > 0:
            for copy in w_copies[t - 1]:
                copy.wait_recv()
        pair = []
        if t < 8:
            piece = shard((place + ring - t) % ring)
            pair.append(remote(wsh if t == 0 else piece, piece, ws.at[0, t], wr.at[0, t], up_id))
        if t < 7:
            piece = shard((place + t) % ring)
            pair.append(remote(wsh if t == 0 else piece, piece, ws.at[1, t], wr.at[1, t], down_id))
        for copy in pair:
            copy.start()
        w_copies.append(pair)

    y_copies = []

    def w_spread():
        for copy in w_copies[7]:
            copy.wait_recv()
        for d in range(1, NY):
            copy = remote(wout.at[c, y], wout.at[c, y], ys.at[d - 1], yr.at[d - 1], {"y": (y + d) % NY})
            copy.start()
            y_copies.append(copy)

    c_copies = []

    def w_sibling(d):
        if d > 0:
            y_copies[d - 1].wait_recv()
        part = wout.at[c, (y + NY - d) % NY, pl.ds(4 * (1 - c), 4)]
        copy = remote(part, part, cs.at[d], cr.at[d], sibling)
        copy.start()
        c_copies.append(copy)

    own.wait()
    spread(0)
    own_w.wait()
    for t in range(3):
        w_step(t)
    order = (0,) + Z_ORDER
    for i in range(1, NZ):
        z_copies[order[i]].wait_recv()
        spread(order[i])
        relay(order[i - 1])
        if i >= 2:
            finish(order[i - 2])
        if i == 1:
            w_step(3)
            w_step(4)
        if i == 2:
            w_step(5)
            w_step(6)
        if i == 3:
            w_step(7)
            w_spread()
            w_sibling(0)
    relay(order[NZ - 1])
    finish(order[NZ - 2])
    for d in range(1, NY):
        w_sibling(d)
    finish(order[NZ - 1])

    for copy in z_copies.values():
        copy.wait_send()
    for s in range(NZ):
        for copy in x_copies[s]:
            copy.wait_send()
        for copy in relay_copies[s]:
            copy.wait_send()
    for pair in w_copies:
        for copy in pair:
            copy.wait_send()
    for copy in y_copies:
        copy.wait_send()
    for copy in c_copies:
        copy.wait()
    count = NX * NZ
    whole = remote(xout.at[pl.ds(base, count)], xout.at[pl.ds(count - base, count)], bs, br, sibling)
    whole.wait()


def exchange(signals, shard):
    rows = signals.shape[0] // NZ
    width = signals.shape[1]
    dma = pltpu.SemaphoreType.DMA
    any_spec = pl.BlockSpec(memory_space=pl.ANY)
    return pl.pallas_call(
        exchange_kernel,
        out_shape=(
            jax.ShapeDtypeStruct((NC * NX * NZ, rows, width), signals.dtype),
            jax.ShapeDtypeStruct((NC, NY, NZ, NH) + shard.shape, shard.dtype),
        ),
        in_specs=[any_spec, any_spec],
        out_specs=(any_spec, any_spec),
        scratch_shapes=[
            dma((2,)),
            dma((NZ - 1,)),
            dma((NZ - 1,)),
            dma((2, NZ)),
            dma((2, NZ)),
            dma((2, 2, NZ)),
            dma,
            dma,
            dma((2, 8)),
            dma((2, 8)),
            dma((NY - 1,)),
            dma((NY - 1,)),
            dma((NY,)),
            dma((NY,)),
        ],
        compiler_params=pltpu.CompilerParams(collective_id=0, has_side_effects=True),
        name="exchange",
    )(signals.reshape(NZ, rows, width), shard)


def product_kernel(scalars, x0, x1, x2, x3, x4, w, out):
    blocks = (x0, x1, x2, x3, x4)
    halves = []
    for part in range(NC):
        total = None
        for k, xk in enumerate(blocks):
            panel = jnp.concatenate(
                [
                    w[cc, yy, 0, hh, 16 * k : 16 * k + 16, :]
                    for hh in range(NH)
                    for yy in range(NY)
                    for cc in range(NC)
                ],
                axis=0,
            )
            term = lax.dot_general(panel, xk[part, 0], (((1,), (1,)), ((), ())), preferred_element_type=jnp.float32)
            total = term if total is None else total + term
        halves.append(total.astype(jnp.bfloat16))
    for k, xk in enumerate(blocks):
        left = jnp.dot(halves[0], xk[0, 0], preferred_element_type=jnp.float32)
        left = left + jnp.dot(halves[1], xk[1, 0], preferred_element_type=jnp.float32)
        left = left.astype(jnp.bfloat16)
        for hh in range(NH):
            for yy in range(NY):
                start = hh * 128 + yy * 32
                out[yy, 0, k, hh] = left[start : start + 32, :]


def products(offsets, blocks, panels):
    count = NX * NZ
    x, c = lax.axis_index("x"), lax.axis_index("c")
    rows, width = blocks.shape[1:]
    lines = x * NZ + 4 * c + jnp.arange(4, dtype=jnp.int32)
    columns = jnp.mod(lines[:, None] + offsets[None, :], count).reshape(-1)
    scalars = jnp.concatenate([columns, 4 * c + jnp.arange(4, dtype=jnp.int32)]).astype(jnp.int32)

    def x_spec(k):
        return pl.BlockSpec((NC, 1, rows, width), lambda j, sc, k=k: (0, sc[5 * j + k], 0, 0))

    shape = (NY, 4, 5, NH, 32, width)
    return pl.pallas_call(
        product_kernel,
        out_shape=jax.ShapeDtypeStruct(shape, jnp.bfloat16),
        grid_spec=pltpu.PrefetchScalarGridSpec(
            num_scalar_prefetch=1,
            grid=(4,),
            in_specs=[x_spec(k) for k in range(5)]
            + [pl.BlockSpec((NC, NY, 1, NH, 80, width), lambda j, sc: (0, 0, sc[20 + j], 0, 0, 0))],
            out_specs=pl.BlockSpec((NY, 1, 5, NH, 32, width), lambda j, sc: (0, j, 0, 0, 0, 0)),
        ),
        compiler_params=pltpu.CompilerParams(vmem_limit_bytes=32 << 20),
        name="products",
    )(scalars, *([blocks.reshape(NC, count, rows, width)] * 5), panels)


def sum_kernel(parts, out, own, yrecv, held, zrecv, own_sem, ys, yr, zs, zr, self_sem):
    zl, zh = lax.axis_index("zl"), lax.axis_index("zh")
    y, c = lax.axis_index("y"), lax.axis_index("c")
    place = zh * NZ + zl
    ring = NH * NZ

    barrier = pltpu.get_barrier_semaphore()
    for d in range(1, NY):
        pl.semaphore_signal(barrier, inc=1, device_id={"y": (y + d) % NY}, device_id_type=MESH)
    me = place * NC + c
    for d in range(1, ring * NC):
        other = (me + d) % (ring * NC)
        pl.semaphore_signal(
            barrier,
            inc=1,
            device_id={"zh": other // (NZ * NC), "zl": (other // NC) % NZ, "c": other % NC},
            device_id_type=MESH,
        )
    pl.semaphore_wait(barrier, NY - 1 + ring * NC - 1)

    load = pltpu.make_async_copy(parts.at[y], own, own_sem)
    load.start()
    y_copies = []
    for i in range(4):
        j = (zl + i) % 4
        line = []
        for d in range(1, NY):
            to = (y + d) % NY
            copy = remote(parts.at[to, j], yrecv.at[d - 1, j], ys.at[i, d - 1], yr.at[i, d - 1], {"y": to})
            copy.start()
            line.append(copy)
        y_copies.append(line)
    load.wait()

    def final(j, hh, cc):
        return remote(
            held.at[j, hh, cc],
            zrecv.at[place],
            zs.at[j, hh, cc],
            zr.at[place],
            {"zl": 4 * c + j, "zh": hh, "c": cc},
        )

    def is_me(j, hh, cc):
        return (4 * c + j == zl) & (hh == zh) & (cc == c)

    for i in range(4):
        j = (zl + i) % 4
        for copy in y_copies[i]:
            copy.wait_recv()
        total = own[j].astype(jnp.float32)
        for d in range(NY - 1):
            total = total + yrecv[d, j].astype(jnp.float32)
        total = total.astype(jnp.bfloat16)
        for hh in range(NH):
            for cc in range(NC):
                held[j, hh, cc] = total[:, hh, 16 * cc : 16 * cc + 16, :]

                @pl.when(is_me(j, hh, cc))
                def _(j=j, hh=hh, cc=cc):
                    copy = pltpu.make_async_copy(held.at[j, hh, cc], zrecv.at[place], self_sem)
                    copy.start()
                    copy.wait()

                @pl.when(jnp.logical_not(is_me(j, hh, cc)))
                def _(j=j, hh=hh, cc=cc):
                    final(j, hh, cc).start()

    source_core = zl // 4
    total = None
    for d in range(ring):
        p = (place + d) % ring

        def wait_one(p=p):
            remote(held.at[0, 0, 0], zrecv.at[p], zs.at[0, 0, 0], zr.at[p], {"c": 1 - c}).wait_recv()

        if d == 0:
            pl.when(source_core != c)(wait_one)
        else:
            wait_one()
        term = zrecv[p].astype(jnp.float32)
        total = term if total is None else total + term
    out[...] = total

    for i in range(4):
        j = (zl + i) % 4
        for copy in y_copies[i]:
            copy.wait_send()
        for hh in range(NH):
            for cc in range(NC):

                @pl.when(jnp.logical_not(is_me(j, hh, cc)))
                def _(j=j, hh=hh, cc=cc):
                    final(j, hh, cc).wait_send()


def tile_sums(parts):
    width = parts.shape[-1]
    dma = pltpu.SemaphoreType.DMA
    bf16 = jnp.bfloat16
    return pl.pallas_call(
        sum_kernel,
        out_shape=jax.ShapeDtypeStruct((5, 16, width), jnp.float32),
        in_specs=[pl.BlockSpec(memory_space=pl.ANY)],
        out_specs=pl.BlockSpec(memory_space=pltpu.VMEM),
        scratch_shapes=[
            pltpu.VMEM((4, 5, NH, 32, width), bf16),
            pltpu.VMEM((NY - 1, 4, 5, NH, 32, width), bf16),
            pltpu.VMEM((4, NH, NC, 5, 16, width), bf16),
            pltpu.VMEM((NH * NZ, 5, 16, width), bf16),
            dma,
            dma((4, NY - 1)),
            dma((4, NY - 1)),
            dma((4, NH, NC)),
            dma((NH * NZ,)),
            dma,
        ],
        compiler_params=pltpu.CompilerParams(collective_id=1, has_side_effects=True, vmem_limit_bytes=32 << 20),
        name="tile_sums",
    )(parts)


def per_device(signals, omega, pattern):
    team_count = NX * NZ
    replica_count = lax.axis_size(REP)
    team_index = lax.axis_index(("x", "zl"))
    replica_index = lax.axis_index(REP)
    slot_count, tile_rows, width = omega.shape[1:]
    time_length = signals.shape[0] * replica_count
    offsets = jnp.mod(pattern[0] - team_index, team_count)

    shard = omega[0].astype(jnp.bfloat16).reshape(slot_count * tile_rows, width)
    blocks, panels = exchange(signals, shard)
    own_terms = tile_sums(products(offsets, blocks, panels))

    flipped = lax.all_to_all(own_terms, REP, 2, 1, tiled=True)
    flipped = jnp.swapaxes(flipped, 1, 2)
    match = offsets[None, :] == jnp.mod(team_count - offsets, team_count)[:, None]
    mirror = jnp.argmax(match, axis=1)
    outgoing = flipped[mirror]
    for level in range(team_count.bit_length() - 1):
        step = 1 << level
        route = [((i + step) % team_count, i) for i in range(team_count)]
        shifted = lax.ppermute(outgoing, ("x", "zl"), route)
        chosen = jnp.mod(offsets // step, 2) == 1
        outgoing = jnp.where(chosen[:, None, None], shifted, outgoing)

    gradient = (own_terms + outgoing) / (2.0 * time_length)
    tiles = omega[0]
    column_ids = jnp.arange(width, dtype=jnp.int32)
    row_ids = replica_index * tile_rows + jnp.arange(tile_rows, dtype=jnp.int32)
    diagonal = column_ids[None, :] == row_ids[:, None]
    diagonal = diagonal[None] & (offsets == 0)[:, None, None]
    gradient = gradient - jnp.where(diagonal, 1.0 / jnp.where(diagonal, tiles, 1.0), 0.0)
    value = tiles - STEP_SIZE * gradient
    shrunk = jnp.sign(value) * jnp.maximum(jnp.abs(value) - STEP_SIZE * PENALTY, 0.0)
    return jnp.where(diagonal, value, shrunk)[None]


def solution(mesh):
    return jax.shard_map(
        per_device,
        mesh=fine_mesh(mesh),
        in_specs=(P(REP, ("x", "zl")), P(("x", "zl"), None, REP, None), P(("x", "zl"), None)),
        out_specs=P(("x", "zl"), None, REP, None),
        check_vma=False,
    )
```

time: 670 us -> 260 us (0.39)
  waiting for transfers between devices: 490 us -> 60.4 us
  Pallas kernels: 0 us -> 160 us
  blocking collectives: 101 us -> 0 us
  local copies, waits for them, and re-layouts: 25 us -> 9.39 us
  between operations: 13.3 us -> 0.18 us
  matrix products: 12.5 us -> 0 us
    reduce_scatter x2 -> x0, waiting for transfers between devices: 303 us -> none  [the longest x1 245 us: per_device(): own_terms = lax.psum_scatter(left, REP, scatter_dimension=2, tiled=True)]
    pallas_call x0 -> x3, Pallas kernels: none -> 160 us  [the longest x1 108 us: exchange(): pl.pallas_call(exchange_kernel, out_shape=(jax.ShapeDtypeStruct((NC * NX...]
    all_gather x2 -> x0, waiting for transfers between devices: 124 us -> none  [the longest x1 114 us: per_device(): panels = lax.all_gather(panels, 'zl', axis=0, tiled=True)]
    all_to_all x1 -> x0, blocking collectives: 55.6 us -> none  [per_device(): blocks = lax.all_to_all(own, 'zl', 0, 0, tiled=True)]
    all_gather x1 -> x0, blocking collectives: 45.3 us -> none  [per_device(): panels = lax.all_gather(omega.astype(jnp.bfloat16), REP, axis=2, tiled=True)]
    dot_general x1 -> x0, matrix products: 12.5 us -> none  [per_device(): jnp.einsum('jtd,jktc->jkdc', mixed, gathered, preferred_element_type=jnp....]
    transpose x1 -> x0, local copies, waits for them, and re-layouts: 11.6 us -> none  [per_device(): jnp.einsum('jtd,jktc->jkdc', mixed, gathered, preferred_element_type=jnp....]
    gather x1 -> x0, local copies, waits for them, and re-layouts: 6.74 us -> none  [per_device(): gathered = blocks[columns]]
  transfers between devices with their start and end apart: 10 -> 6, of which waited for: 10 -> 6; matrix products, arithmetic and copies ran while one was open for 1% -> 0% of each run, Pallas kernels for 0% -> 0%
where the time goes in v2:
time: 260 us; the launch traced here: 259 us
  Pallas kernels  160 us (62%)
  waiting for transfers between devices  60.4 us (23%)
  starting transfers between devices  24.2 us (9%)
  local copies, waits for them, and re-layouts  9.39 us (4%)
  other arithmetic  5.09 us (2%)
    pallas_call x1, Pallas kernels, exchange(): pl.pallas_call(exchange_kernel, out_shape=(jax.ShapeDtypeStruct((NC * NX...  108 us
    pallas_call x1, Pallas kernels, tile_sums(): pl.pallas_call(sum_kernel, out_shape=jax.ShapeDtypeStruct((5, 16, width),...  46.6 us
    ppermute x5, waiting for transfers between devices, per_device(): shifted = lax.ppermute(outgoing, ('x', 'zl'), route)  46.1 us
    all_to_all x1, waiting for transfers between devices, per_device(): flipped = lax.all_to_all(own_terms, REP, 2, 1, tiled=True)  14.3 us
    all_to_all x1, starting transfers between devices, per_device(): flipped = lax.all_to_all(own_terms, REP, 2, 1, tiled=True)  13.5 us
    ppermute x5, starting transfers between devices, per_device(): shifted = lax.ppermute(outgoing, ('x', 'zl'), route)  10.6 us
    unnamed x10, local copies, waits for them, and re-layouts  7.17 us
    pallas_call x1, Pallas kernels, products(): pl.pallas_call(product_kernel, out_shape=jax.ShapeDtypeStruct(shape, jnp....  5.85 us
  transfers between devices with their start and end apart: 6, of which 6 were waited for; matrix products, arithmetic and copies ran while one was open for 0% of the time, Pallas kernels for 0%

profile of v2, /device:TPU:230, one launch (start us, length us, event | category | flops | bytes accessed | tf_op | source)
XLA Modules:
  0.0 259.4 jit_solution(4123618528053890495)
XLA Ops:
  0.0 0.7 fusion.5
  0.8 1.5 convert_element_type.7
  2.4 107.7 %exchange.1 = (bf16[64,256,256]{2,1,0:T(8,128)(2,1)}, bf16[2,4,8,2,80,256]{5,4,3,2,1,0:T(8,128)(2,1)}) custom-call(bf16[8,256,256]{2,1,0:T(8,128)(2,1)} %bitcast.33, bf16[80,256]{1,0:T(8,128)(2,1)} %bitcast.35), custom_call_target="tpu_custom_call" | custom-call | tf_op jit(solution)/shard_map/exchange/pallas_call | solution.py:198
  110.2 3.4 %copy-done = bf16[64,256,256]{2,1,0:T(8,128)(2,1)S(1)} copy-done((bf16[64,256,256]{2,1,0:T(8,128)(2,1)S(1)}, bf16[64,256,256]{2,1,0:T(8,128)(2,1)}, u32[]{:S(2)}) %copy-start) | copy-done | bytes 8388632
  113.5 2.5 copy-done.1
  116.0 5.9 %products.1.parts = bf16[4,4,5,2,32,256]{5,4,3,2,1,0:T(8,128)(2,1)S(1)} custom-call(s32[24]{0:T(128)S(1)} %pad_add_fusion.scalars, bf16[2,32,256,256]{3,2,1,0:T(8,128)(2,1)S(1)} %bitcast.25, bf16[2,32,256,256]{3,2,1,0:T(8,128)(2,1)S(1)} %bitcast.26, bf16[2,32,256,256]{3,2,1,0:T(8,128)(2,1)S(1)} %bitcast.27, bf16[2,32,256,256]{3,2,1,0:T(8,128)(2,1)S(1)} %bitcast.28, ...), custom_call_target="tpu_custom_call" | custom-call | tf_op jit(solution)/shard_map/products/pallas_call | solution.py:267
  121.9 46.6 %tile_sums.1 = f32[5,16,256]{2,1,0:T(8,128)S(1)} custom-call(bf16[4,4,5,2,32,256]{5,4,3,2,1,0:T(8,128)(2,1)S(1)} %products.1.parts), custom_call_target="tpu_custom_call" | custom-call | tf_op jit(solution)/shard_map/tile_sums/pallas_call | solution.py:382
  168.9 1.0 reshape.218
  169.9 13.5 %all-to-all-start = ((f32[16,1,1280]{2,1,0:T(1,128)}), f32[16,1,1280]{2,1,0:T(1,128)S(1)}, u32[]{:S(2)}, u32[]{:S(2)}) async-start(f32[16,1,1280]{2,1,0:T(1,128)} %reshape.218), calls=%async_computation | async-start | bytes 163840 | tf_op jit(solution)/shard_map/all_to_all | solution.py:417
  183.5 0.7 iota_reduce_fusion
  184.2 14.3 %all-to-all-done = f32[16,1,1280]{2,1,0:T(1,128)S(1)} async-done(((f32[16,1,1280]{2,1,0:T(1,128)}), f32[16,1,1280]{2,1,0:T(1,128)S(1)}, u32[]{:S(2)}, u32[]{:S(2)}) %all-to-all-start) | async-done | bytes 81952 | tf_op jit(solution)/shard_map/all_to_all | solution.py:417
  199.0 0.8 reduce.19
  200.9 0.6 gather_fusion
  201.4 3.0 %collective-permute-start = (f32[5,16,256]{2,1,0:T(8,128)S(1)}, f32[5,16,256]{2,1,0:T(8,128)S(1)}, u32[]{:S(2)}, u32[]{:S(2)}) collective-permute-start(f32[5,16,256]{2,1,0:T(8,128)S(1)} %gather_fusion), channel_id=1, source_target_pairs={{16,0},{32,16},{48,32},{64,48},{80,64},{96,80},{112,96},{128,112},... | collective-permute-start | bytes 245768 | tf_op jit(solution)/shard_map/ppermute | solution.py:425
  204.5 12.0 %collective-permute-done = f32[5,16,256]{2,1,0:T(8,128)S(1)} collective-permute-done((f32[5,16,256]{2,1,0:T(8,128)S(1)}, f32[5,16,256]{2,1,0:T(8,128)S(1)}, u32[]{:S(2)}, u32[]{:S(2)}) %collective-permute-start) | collective-permute-done | bytes 81952 | tf_op jit(solution)/shard_map/ppermute | solution.py:425
  216.6 1.9 collective-permute-start.1
  218.5 12.2 %collective-permute-done.1 = f32[5,16,256]{2,1,0:T(8,128)S(1)} collective-permute-done((f32[5,16,256]{2,1,0:T(8,128)S(1)}, f32[5,16,256]{2,1,0:T(8,128)S(1)}, u32[]{:S(2)}, u32[]{:S(2)}) %collective-permute-start.1) | collective-permute-done | bytes 81952 | tf_op jit(solution)/shard_map/ppermute | solution.py:425
  230.8 1.9 collective-permute-start.2
  232.7 10.4 %collective-permute-done.2 = f32[5,16,256]{2,1,0:T(8,128)S(1)} collective-permute-done((f32[5,16,256]{2,1,0:T(8,128)S(1)}, f32[5,16,256]{2,1,0:T(8,128)S(1)}, u32[]{:S(2)}, u32[]{:S(2)}) %collective-permute-start.2) | collective-permute-done | bytes 81952 | tf_op jit(solution)/shard_map/ppermute | solution.py:425
  243.2 1.9 collective-permute-start.3
  245.1 5.6 %collective-permute-done.3 = f32[5,16,256]{2,1,0:T(8,128)S(1)} collective-permute-done((f32[5,16,256]{2,1,0:T(8,128)S(1)}, f32[5,16,256]{2,1,0:T(8,128)S(1)}, u32[]{:S(2)}, u32[]{:S(2)}) %collective-permute-start.3) | collective-permute-done | bytes 81952 | tf_op jit(solution)/shard_map/ppermute | solution.py:425
  250.8 1.9 collective-permute-start.4
  252.8 5.8 %collective-permute-done.4 = f32[5,16,256]{2,1,0:T(8,128)S(1)} collective-permute-done((f32[5,16,256]{2,1,0:T(8,128)S(1)}, f32[5,16,256]{2,1,0:T(8,128)S(1)}, u32[]{:S(2)}, u32[]{:S(2)}) %collective-permute-start.4) | collective-permute-done | bytes 81952 | tf_op jit(solution)/shard_map/ppermute | solution.py:425
  258.6 0.8 fusion.4
  (28 shorter events, 2.6 us)
Async XLA Ops:
  110.2 3.4 %copy-start = (bf16[64,256,256]{2,1,0:T(8,128)(2,1)S(1)}, bf16[64,256,256]{2,1,0:T(8,128)(2,1)}, u32[]{:S(2)}) copy-start(bf16[64,256,256]{2,1,0:T(8,128)(2,1)} %get-tuple-element.8) | copy-start | bytes 25165828
  113.5 2.5 copy-start.1
  116.0 67.4 %copy-start.3 = (s32[1,5]{1,0:T(1,128)S(1)}, s32[1,5]{1,0:T(1,128)}, u32[]{:S(2)}) copy-start(s32[1,5]{1,0:T(1,128)} %param.5) | copy-start | bytes 64
  121.9 136.7 %copy-start.2 = (f32[1,5,16,256]{3,2,1,0:T(8,128)S(1)}, f32[1,5,16,256]{3,2,1,0:T(8,128)}, u32[]{:S(2)}) copy-start(f32[1,5,16,256]{3,2,1,0:T(8,128)} %param.4) | copy-start | bytes 245764
  169.9 28.6 %all-to-all-start = ((f32[16,1,1280]{2,1,0:T(1,128)}), f32[16,1,1280]{2,1,0:T(1,128)S(1)}, u32[]{:S(2)}, u32[]{:S(2)}) async-start(f32[16,1,1280]{2,1,0:T(1,128)} %reshape.218), calls=%async_computation | async-start | bytes 163840 | tf_op jit(solution)/shard_map/all_to_all | solution.py:417
  201.4 15.0 %collective-permute-start = (f32[5,16,256]{2,1,0:T(8,128)S(1)}, f32[5,16,256]{2,1,0:T(8,128)S(1)}, u32[]{:S(2)}, u32[]{:S(2)}) collective-permute-start(f32[5,16,256]{2,1,0:T(8,128)S(1)} %gather_fusion), channel_id=1, source_target_pairs={{16,0},{32,16},{48,32},{64,48},{80,64},{96,80},{112,96},{128,112},... | collective-permute-start | bytes 245768 | tf_op jit(solution)/shard_map/ppermute | solution.py:425
  216.6 14.1 %collective-permute-start.1 = (f32[5,16,256]{2,1,0:T(8,128)S(1)}, f32[5,16,256]{2,1,0:T(8,128)S(1)}, u32[]{:S(2)}, u32[]{:S(2)}) collective-permute-start(f32[5,16,256]{2,1,0:T(8,128)S(1)} %broadcast_select_fusion), channel_id=1, source_target_pairs={{32,0},{48,16},{64,32},{80,48},{96,64},{112,80},{128,96},{144,112}... | collective-permute-start | bytes 245768 | tf_op jit(solution)/shard_map/ppermute | solution.py:425
  230.8 12.3 %collective-permute-start.2 = (f32[5,16,256]{2,1,0:T(8,128)S(1)}, f32[5,16,256]{2,1,0:T(8,128)S(1)}, u32[]{:S(2)}, u32[]{:S(2)}) collective-permute-start(f32[5,16,256]{2,1,0:T(8,128)S(1)} %broadcast_select_fusion.1), channel_id=1, source_target_pairs={{64,0},{80,16},{96,32},{112,48},{128,64},{144,80},{160,96},{176,11... | collective-permute-start | bytes 245768 | tf_op jit(solution)/shard_map/ppermute | solution.py:425
  243.2 7.5 %collective-permute-start.3 = (f32[5,16,256]{2,1,0:T(8,128)S(1)}, f32[5,16,256]{2,1,0:T(8,128)S(1)}, u32[]{:S(2)}, u32[]{:S(2)}) collective-permute-start(f32[5,16,256]{2,1,0:T(8,128)S(1)} %broadcast_select_fusion.2), channel_id=1, source_target_pairs={{128,0},{144,16},{160,32},{176,48},{192,64},{208,80},{224,96},{240... | collective-permute-start | bytes 245768 | tf_op jit(solution)/shard_map/ppermute | solution.py:425
  250.8 7.8 %collective-permute-start.4 = (f32[5,16,256]{2,1,0:T(8,128)S(1)}, f32[5,16,256]{2,1,0:T(8,128)S(1)}, u32[]{:S(2)}, u32[]{:S(2)}) collective-permute-start(f32[5,16,256]{2,1,0:T(8,128)S(1)} %broadcast_select_fusion.3), channel_id=1, source_target_pairs={{256,0},{272,16},{288,32},{304,48},{320,64},{336,80},{352,96},{368... | collective-permute-start | bytes 245768 | tf_op jit(solution)/shard_map/ppermute | solution.py:425

commit v3 on v2

--- a/solution.py
+++ b/solution.py
@@ -11,7 +11,6 @@
 REP = ("zh", "y", "c")
 MESH = pl.DeviceIdType.MESH
 NX, NZ, NH, NY, NC = 4, 8, 2, 4, 2
-Z_ORDER = (4, 5, 6, 7, 1, 2, 3)
 
 
 def fine_mesh(mesh):
@@ -33,7 +32,7 @@
 
 
 def exchange_kernel(
-    sig, wsh, xout, wout, local_sem, zs, zr, xs_sem, xr, rs, bs, br, ws, wr, ys, yr, cs, cr
+    sig, wsh, xout, wout, local_sem, zs, zr, xs_sem, xr, rs, bs, br, ws, wr, ys, yr, qs, qr, cs, cr
 ):
     x, zl, zh = lax.axis_index("x"), lax.axis_index("zl"), lax.axis_index("zh")
     y, c = lax.axis_index("y"), lax.axis_index("c")
@@ -59,11 +58,15 @@
     own_w = pltpu.make_async_copy(wsh, wout.at[c, y, zl, zh], local_sem.at[1])
     own_w.start()
     z_copies = {}
-    for s in Z_ORDER:
+
+    def z_start(s):
         peer = flip(zl, s)
         copy = remote(sig.at[peer], xout.at[mine], zs.at[s - 1], zr.at[s - 1], {"zl": peer})
         copy.start()
         z_copies[s] = copy
+
+    for s in (4, 1, 2, 3, 5):
+        z_start(s)
 
     def block(dx, s):
         return base + ((x + dx) % NX) * NZ + flip(zl, s)
@@ -103,73 +106,90 @@
             copy.wait_recv()
         to_sibling(block(2, s))
 
-    def shard(origin):
-        return wout.at[c, y, origin % NZ, origin // NZ]
-
-    w_copies = []
-
-    def w_step(t):
-        if t > 0:
-            for copy in w_copies[t - 1]:
-                copy.wait_recv()
-        pair = []
-        if t < 8:
-            piece = shard((place + ring - t) % ring)
-            pair.append(remote(wsh if t == 0 else piece, piece, ws.at[0, t], wr.at[0, t], up_id))
+    def origin(e):
+        return (place + ring - (e + 1) // 2) % ring if e % 2 else (place + e // 2) % ring
+
+    def shard(e, dy=0):
+        o = origin(e)
+        return wout.at[c, (y + dy) % NY, o % NZ, o // NZ]
+
+    ring_copies = {}
+
+    def w_ring(t):
+        for way, e, steps, where in ((0, max(2 * t - 1, 0), 8, up_id), (1, 2 * t, 7, down_id)):
+            if t < steps:
+                piece = shard(e)
+                copy = remote(wsh if t == 0 else piece, piece, ws.at[way, t], wr.at[way, t], where)
+                copy.start()
+                ring_copies[way, t] = copy
+
+    forward, backward = {"y": (y + 1) % NY}, {"y": (y + NY - 1) % NY}
+    y_copies, y_relays = {}, {}
+
+    def w_forward(e):
+        here = shard(e)
+        for way, where in enumerate((forward, backward)):
+            copy = remote(here, here, ys.at[way, e], yr.at[way, e], where)
+            copy.start()
+            y_copies[way, e] = copy
+
+    def w_relay(e):
+        for way, (dy, start, size, where) in enumerate(((NY - 1, 0, 48, forward), (1, 48, 32, backward))):
+            y_copies[way, e].wait_recv()
+            part = shard(e, dy).at[pl.ds(start, size)]
+            copy = remote(part, part, qs.at[way, e], qr.at[way, e], where)
+            copy.start()
+            y_relays[way, e] = copy
+
+    def w_pass(t):
+        for way in range(2):
+            if (way, t) in ring_copies:
+                ring_copies[way, t].wait_recv()
         if t < 7:
-            piece = shard((place + t) % ring)
-            pair.append(remote(wsh if t == 0 else piece, piece, ws.at[1, t], wr.at[1, t], down_id))
-        for copy in pair:
-            copy.start()
-        w_copies.append(pair)
-
-    y_copies = []
-
-    def w_spread():
-        for copy in w_copies[7]:
-            copy.wait_recv()
-        for d in range(1, NY):
-            copy = remote(wout.at[c, y], wout.at[c, y], ys.at[d - 1], yr.at[d - 1], {"y": (y + d) % NY})
-            copy.start()
-            y_copies.append(copy)
+            w_ring(t + 1)
+        for way, e in ((0, 2 * t + 1), (1, 2 * t + 2)):
+            if (way, t) in ring_copies:
+                w_forward(e)
+
+    def w_relays(t):
+        for e in (0,) if t < 0 else (2 * t + 1, 2 * t + 2):
+            if (0, e) in y_copies:
+                w_relay(e)
 
     c_copies = []
 
-    def w_sibling(d):
-        if d > 0:
-            y_copies[d - 1].wait_recv()
-        part = wout.at[c, (y + NY - d) % NY, pl.ds(4 * (1 - c), 4)]
-        copy = remote(part, part, cs.at[d], cr.at[d], sibling)
+    def w_sibling(dy):
+        part = wout.at[c, (y + dy) % NY, pl.ds(4 * (1 - c), 4)]
+        copy = remote(part, part, cs.at[dy], cr.at[dy], sibling)
         copy.start()
         c_copies.append(copy)
 
+    w_ring(0)
     own.wait()
     spread(0)
     own_w.wait()
-    for t in range(3):
-        w_step(t)
-    order = (0,) + Z_ORDER
+    w_forward(0)
     for i in range(1, NZ):
-        z_copies[order[i]].wait_recv()
-        spread(order[i])
-        relay(order[i - 1])
+        z_copies[i].wait_recv()
+        if i + 2 in (6, 7):
+            z_start(i + 2)
+        spread(i)
+        relay(i - 1)
         if i >= 2:
-            finish(order[i - 2])
-        if i == 1:
-            w_step(3)
-            w_step(4)
-        if i == 2:
-            w_step(5)
-            w_step(6)
-        if i == 3:
-            w_step(7)
-            w_spread()
-            w_sibling(0)
-    relay(order[NZ - 1])
-    finish(order[NZ - 2])
-    for d in range(1, NY):
-        w_sibling(d)
-    finish(order[NZ - 1])
+            finish(i - 2)
+        w_pass(i - 1)
+        w_relays(i - 2)
+    relay(NZ - 1)
+    w_pass(NZ - 1)
+    finish(NZ - 2)
+    w_sibling(0)
+    w_relays(NZ - 2)
+    finish(NZ - 1)
+    w_relays(NZ - 1)
+    for copy in y_relays.values():
+        copy.wait_recv()
+    for dy in range(1, NY):
+        w_sibling(dy)
 
     for copy in z_copies.values():
         copy.wait_send()
@@ -178,11 +198,9 @@
             copy.wait_send()
         for copy in relay_copies[s]:
             copy.wait_send()
-    for pair in w_copies:
-        for copy in pair:
+    for group in (ring_copies, y_copies, y_relays):
+        for copy in group.values():
             copy.wait_send()
-    for copy in y_copies:
-        copy.wait_send()
     for copy in c_copies:
         copy.wait()
     count = NX * NZ
@@ -214,8 +232,10 @@
             dma,
             dma((2, 8)),
             dma((2, 8)),
-            dma((NY - 1,)),
-            dma((NY - 1,)),
+            dma((2, 16)),
+            dma((2, 16)),
+            dma((2, 16)),
+            dma((2, 16)),
             dma((NY,)),
             dma((NY,)),
         ],
@@ -274,30 +294,51 @@
             + [pl.BlockSpec((NC, NY, 1, NH, 80, width), lambda j, sc: (0, 0, sc[20 + j], 0, 0, 0))],
             out_specs=pl.BlockSpec((NY, 1, 5, NH, 32, width), lambda j, sc: (0, j, 0, 0, 0, 0)),
         ),
-        compiler_params=pltpu.CompilerParams(vmem_limit_bytes=32 << 20),
+        compiler_params=pltpu.CompilerParams(vmem_limit_bytes=60 << 20),
         name="products",
     )(scalars, *([blocks.reshape(NC, count, rows, width)] * 5), panels)
 
 
-def sum_kernel(parts, out, own, yrecv, held, zrecv, own_sem, ys, yr, zs, zr, self_sem):
-    zl, zh = lax.axis_index("zl"), lax.axis_index("zh")
+def update_kernel(
+    pattern, parts, tiles, out, own, yrecv, held, zrecv, msgs, turned, sent, got,
+    own_sem, ys, yr, zs, zr, self_sem, ts, tr, hs, hr
+):
+    x, zl, zh = lax.axis_index("x"), lax.axis_index("zl"), lax.axis_index("zh")
     y, c = lax.axis_index("y"), lax.axis_index("c")
     place = zh * NZ + zl
     ring = NH * NZ
+    team = x * NZ + zl
+    teams = NX * NZ
+    rep = (zh * NY + y) * NC + c
+    reps = NH * NY * NC
+    source_core = zl // 4
+
+    def rep_id(r):
+        return {"zh": r // (NY * NC), "y": (r // NC) % NY, "c": r % NC}
+
+    def team_id(t):
+        return {"x": t // NZ, "zl": t % NZ}
+
+    def greet(where):
+        pl.semaphore_signal(barrier, inc=1, device_id=where, device_id_type=MESH)
 
     barrier = pltpu.get_barrier_semaphore()
     for d in range(1, NY):
-        pl.semaphore_signal(barrier, inc=1, device_id={"y": (y + d) % NY}, device_id_type=MESH)
-    me = place * NC + c
-    for d in range(1, ring * NC):
-        other = (me + d) % (ring * NC)
-        pl.semaphore_signal(
-            barrier,
-            inc=1,
-            device_id={"zh": other // (NZ * NC), "zl": (other // NC) % NZ, "c": other % NC},
-            device_id_type=MESH,
-        )
-    pl.semaphore_wait(barrier, NY - 1 + ring * NC - 1)
+        greet({"y": (y + d) % NY})
+    for d in range(ring):
+        p = (place + d) % ring
+        where = {"zh": p // NZ, "zl": p % NZ, "c": source_core}
+        if d == 0:
+            pl.when(source_core != c)(lambda where=where: greet(where))
+        else:
+            greet(where)
+    for d in range(1, reps):
+        greet(rep_id((rep + d) % reps))
+    for level in range(4):
+        for step in (1 << level, teams - (1 << level)):
+            greet(team_id((team + step) % teams))
+    greetings = NY - 1 + ring - 1 + reps - 1 + 8
+    pl.semaphore_wait(barrier, greetings + jnp.where(source_core != c, 1, 0))
 
     load = pltpu.make_async_copy(parts.at[y], own, own_sem)
     load.start()
@@ -347,7 +388,6 @@
                 def _(j=j, hh=hh, cc=cc):
                     final(j, hh, cc).start()
 
-    source_core = zl // 4
     total = None
     for d in range(ring):
         p = (place + d) % ring
@@ -361,7 +401,87 @@
             wait_one()
         term = zrecv[p].astype(jnp.float32)
         total = term if total is None else total + term
-    out[...] = total
+
+    slots = total.shape[0]
+    lane = lax.broadcasted_iota(jnp.int32, (16, 128), 1) // 16
+    for r in range(reps):
+        message = jnp.zeros((16, 128), jnp.float32)
+        for k in range(slots):
+            piece = total[k, :, 128 * (r // 8) : 128 * (r // 8) + 128]
+            shift = (16 * k - 16 * (r % 8)) % 128
+            if shift:
+                piece = pltpu.roll(piece, shift, 1)
+            message = jnp.where(lane == k, piece, message)
+        msgs[r] = message
+    turn_copies = []
+    for d in range(1, reps):
+        r = (rep + d) % reps
+        copy = remote(msgs.at[r], turned.at[rep], ts.at[d - 1], tr.at[d - 1], rep_id(r))
+        copy.start()
+        turn_copies.append(copy)
+    turned[rep] = msgs[rep]
+    for copy in turn_copies:
+        copy.wait_recv()
+    flipped = jnp.transpose(turned[...].reshape(16 * reps, 128))
+    flipped = [flipped[16 * k : 16 * k + 16] for k in range(slots)]
+
+    offset = [(pattern[0, k] - team + teams) % teams for k in range(slots)]
+    low = [offset[k] < teams // 2 for k in range(slots)]
+    size = [jnp.where(low[k], offset[k], teams - offset[k]) for k in range(slots)]
+    first = [size[k] == size[1] for k in range(slots)]
+
+    def pick(values, is_low, is_first):
+        chosen = values[slots - 1]
+        for k in range(1, slots - 1):
+            chosen = jnp.where((low[k] == is_low) & (first[k] == is_first), values[k], chosen)
+        return chosen
+
+    sizes = [size[1], pick(size, True, False)]
+    ways = []
+    for way in range(2):
+        ways.append([pick(flipped, way == 1, u == 0) for u in range(2)])
+    hops = []
+    for level in range(4):
+        step = 1 << level
+        pair = []
+        for way in range(2):
+            for u in range(2):
+                sent[level, way, u] = ways[way][u]
+            to = (team + (teams - step if way == 0 else step)) % teams
+            copy = remote(
+                sent.at[level, way], got.at[level, way], hs.at[level, way], hr.at[level, way], team_id(to)
+            )
+            copy.start()
+            pair.append(copy)
+        for way in range(2):
+            pair[way].wait_recv()
+            for u in range(2):
+                bit = (sizes[u] // step) % 2 == 1
+                ways[way][u] = jnp.where(bit, got[level, way, u], ways[way][u])
+        hops.append(pair)
+
+    length = 32768.0
+    column = lax.broadcasted_iota(jnp.int32, (16, 256), 1)
+    row = lax.broadcasted_iota(jnp.int32, (16, 256), 0) + rep * 16
+    diagonal = column == row
+    for k in range(slots):
+        tile = tiles[0, k]
+        if k == 0:
+            back = flipped[0]
+        else:
+            one = jnp.where(first[k], ways[0][0], ways[0][1])
+            two = jnp.where(first[k], ways[1][0], ways[1][1])
+            back = jnp.where(low[k], one, two)
+        gradient = (total[k] + back) / (2.0 * length)
+        if k == 0:
+            inverse = 1.0 / jnp.where(diagonal, tile, 1.0)
+            gradient = gradient - jnp.where(diagonal, inverse, 0.0)
+        value = tile - STEP_SIZE * gradient
+        limit = STEP_SIZE * PENALTY
+        shrunk = jnp.where(value > limit, value - limit, jnp.where(value < -limit, value + limit, 0.0))
+        if k == 0:
+            shrunk = jnp.where(diagonal, value, shrunk)
+        out[0, k] = shrunk
 
     for i in range(4):
         j = (zl + i) % 4
@@ -373,69 +493,61 @@
                 @pl.when(jnp.logical_not(is_me(j, hh, cc)))
                 def _(j=j, hh=hh, cc=cc):
                     final(j, hh, cc).wait_send()
-
-
-def tile_sums(parts):
+    for copy in turn_copies:
+        copy.wait_send()
+    for pair in hops:
+        for copy in pair:
+            copy.wait_send()
+
+
+def update(pattern, parts, tiles):
     width = parts.shape[-1]
     dma = pltpu.SemaphoreType.DMA
-    bf16 = jnp.bfloat16
+    bf16, f32 = jnp.bfloat16, jnp.float32
+    reps = NH * NY * NC
     return pl.pallas_call(
-        sum_kernel,
-        out_shape=jax.ShapeDtypeStruct((5, 16, width), jnp.float32),
-        in_specs=[pl.BlockSpec(memory_space=pl.ANY)],
+        update_kernel,
+        out_shape=jax.ShapeDtypeStruct(tiles.shape, f32),
+        in_specs=[
+            pl.BlockSpec(memory_space=pltpu.SMEM),
+            pl.BlockSpec(memory_space=pl.ANY),
+            pl.BlockSpec(memory_space=pltpu.VMEM),
+        ],
         out_specs=pl.BlockSpec(memory_space=pltpu.VMEM),
         scratch_shapes=[
             pltpu.VMEM((4, 5, NH, 32, width), bf16),
             pltpu.VMEM((NY - 1, 4, 5, NH, 32, width), bf16),
             pltpu.VMEM((4, NH, NC, 5, 16, width), bf16),
             pltpu.VMEM((NH * NZ, 5, 16, width), bf16),
+            pltpu.VMEM((reps, 16, 128), f32),
+            pltpu.VMEM((reps, 16, 128), f32),
+            pltpu.VMEM((4, 2, 2, 16, width), f32),
+            pltpu.VMEM((4, 2, 2, 16, width), f32),
             dma,
             dma((4, NY - 1)),
             dma((4, NY - 1)),
             dma((4, NH, NC)),
             dma((NH * NZ,)),
             dma,
+            dma((reps - 1,)),
+            dma((reps - 1,)),
+            dma((4, 2)),
+            dma((4, 2)),
         ],
         compiler_params=pltpu.CompilerParams(collective_id=1, has_side_effects=True, vmem_limit_bytes=32 << 20),
-        name="tile_sums",
-    )(parts)
+        name="update",
+    )(pattern, parts, tiles)
 
 
 def per_device(signals, omega, pattern):
     team_count = NX * NZ
-    replica_count = lax.axis_size(REP)
     team_index = lax.axis_index(("x", "zl"))
-    replica_index = lax.axis_index(REP)
     slot_count, tile_rows, width = omega.shape[1:]
-    time_length = signals.shape[0] * replica_count
     offsets = jnp.mod(pattern[0] - team_index, team_count)
 
     shard = omega[0].astype(jnp.bfloat16).reshape(slot_count * tile_rows, width)
     blocks, panels = exchange(signals, shard)
-    own_terms = tile_sums(products(offsets, blocks, panels))
-
-    flipped = lax.all_to_all(own_terms, REP, 2, 1, tiled=True)
-    flipped = jnp.swapaxes(flipped, 1, 2)
-    match = offsets[None, :] == jnp.mod(team_count - offsets, team_count)[:, None]
-    mirror = jnp.argmax(match, axis=1)
-    outgoing = flipped[mirror]
-    for level in range(team_count.bit_length() - 1):
-        step = 1 << level
-        route = [((i + step) % team_count, i) for i in range(team_count)]
-        shifted = lax.ppermute(outgoing, ("x", "zl"), route)
-        chosen = jnp.mod(offsets // step, 2) == 1
-        outgoing = jnp.where(chosen[:, None, None], shifted, outgoing)
-
-    gradient = (own_terms + outgoing) / (2.0 * time_length)
-    tiles = omega[0]
-    column_ids = jnp.arange(width, dtype=jnp.int32)
-    row_ids = replica_index * tile_rows + jnp.arange(tile_rows, dtype=jnp.int32)
-    diagonal = column_ids[None, :] == row_ids[:, None]
-    diagonal = diagonal[None] & (offsets == 0)[:, None, None]
-    gradient = gradient - jnp.where(diagonal, 1.0 / jnp.where(diagonal, tiles, 1.0), 0.0)
-    value = tiles - STEP_SIZE * gradient
-    shrunk = jnp.sign(value) * jnp.maximum(jnp.abs(value) - STEP_SIZE * PENALTY, 0.0)
-    return jnp.where(diagonal, value, shrunk)[None]
+    return update(pattern, products(offsets, blocks, panels), omega)
 
 
 def solution(mesh):

time: 260 us -> 194 us (0.75)
  the two profiles are of different devices: /device:TPU:230 before, /device:TPU:24 now
where the time goes in v3:
time: 194 us
  Pallas kernels  188 us (97%)
  other arithmetic  2.86 us (1%)
  local copies, waits for them, and re-layouts  2.47 us (1%)
    pallas_call x1, Pallas kernels, exchange(): pl.pallas_call(exchange_kernel, out_shape=(jax.ShapeDtypeStruct((NC * NX...  92.1 us
    pallas_call x1, Pallas kernels, update(): pl.pallas_call(update_kernel, out_shape=jax.ShapeDtypeStruct(tiles.shape,...  87.7 us
    pallas_call x1, Pallas kernels, products(): pl.pallas_call(product_kernel, out_shape=jax.ShapeDtypeStruct(shape, jnp....  8.44 us

profile of v3, /device:TPU:24, one launch (start us, length us, event | category | flops | bytes accessed | tf_op | source)
XLA Modules:
  0.0 193.6 jit_solution(8702762331624515510)
XLA Ops:
  0.0 0.7 fusion
  0.7 0.1 broadcast_add_fusion
  0.8 0.1 add.64
  0.8 0.6 pad_add_fusion.scalars
  1.4 1.5 convert_element_type.7
  3.0 92.1 %exchange.1 = (bf16[64,256,256]{2,1,0:T(8,128)(2,1)}, bf16[2,4,8,2,80,256]{5,4,3,2,1,0:T(8,128)(2,1)}) custom-call(bf16[8,256,256]{2,1,0:T(8,128)(2,1)} %bitcast.10, bf16[80,256]{1,0:T(8,128)(2,1)} %bitcast.11), custom_call_target="tpu_custom_call" | custom-call | tf_op jit(solution)/shard_map/exchange/pallas_call | solution.py:216
  95.1 0.0 copy-start.1
  95.1 0.0 copy-start.2
  95.1 8.4 %products.1.parts = bf16[4,4,5,2,32,256]{5,4,3,2,1,0:T(8,128)(2,1)} custom-call(s32[24]{0:T(128)} %pad_add_fusion.scalars, bf16[2,32,256,256]{3,2,1,0:T(8,128)(2,1)} %bitcast.5, bf16[2,32,256,256]{3,2,1,0:T(8,128)(2,1)} %bitcast.6, bf16[2,32,256,256]{3,2,1,0:T(8,128)(2,1)} %bitcast.7, bf16[2,32,256,256]{3,2,1,0:T(8,128)(2,1)} %bitcast.8, ...), custom_call_target="tpu_custom_call" | custom-call | tf_op jit(solution)/shard_map/products/pallas_call | solution.py:287
  103.5 0.0 copy-done.1
  103.5 0.0 copy-done.2
  103.5 0.0 copy-start
  103.5 1.7 copy-done
  105.3 87.7 %update.1 = f32[1,5,16,256]{3,2,1,0:T(8,128)S(1)} custom-call(s32[1,5]{1,0:T(1,128)S(1)} %copy-done.2, bf16[4,4,5,2,32,256]{5,4,3,2,1,0:T(8,128)(2,1)S(1)} %copy-done, f32[1,5,16,256]{3,2,1,0:T(8,128)S(1)} %copy-done.1), custom_call_target="tpu_custom_call" | custom-call | tf_op jit(solution)/shard_map/update/pallas_call | solution.py:508
  193.0 0.6 copy.5
  (3 shorter events, 0.0 us)
Async XLA Ops:
  95.1 8.5 %copy-start.1 = (f32[1,5,16,256]{3,2,1,0:T(8,128)S(1)}, f32[1,5,16,256]{3,2,1,0:T(8,128)}, u32[]{:S(2)}) copy-start(f32[1,5,16,256]{3,2,1,0:T(8,128)} %tiles.1) | copy-start | bytes 245764
  95.1 8.5 %copy-start.2 = (s32[1,5]{1,0:T(1,128)S(1)}, s32[1,5]{1,0:T(1,128)}, u32[]{:S(2)}) copy-start(s32[1,5]{1,0:T(1,128)} %pattern.1) | copy-start | bytes 64
  103.5 1.7 copy-start

commit v4 on v3

v4 whole, which is shorter than its diff:
```python
import jax
import jax.numpy as jnp
from jax import lax
from jax.experimental import pallas as pl
from jax.experimental.pallas import tpu as pltpu
from jax.sharding import Mesh
from jax.sharding import PartitionSpec as P

STEP_SIZE = 0.5
PENALTY = 0.1
REP = ("zh", "y", "c")
MESH = pl.DeviceIdType.MESH
NX, NZ, NH, NY, NC = 4, 8, 2, 4, 2


def fine_mesh(mesh):
    return Mesh(mesh.devices.reshape(NX, NZ, NH, NY, NC), ("x", "zl", "zh", "y", "c"))


def flip(value, bits):
    for level in range(3):
        weight = 1 << level
        if bits & weight:
            value = value + weight * (1 - 2 * ((value // weight) % 2))
    return value


def remote(src, dst, send, recv, where):
    return pltpu.make_async_remote_copy(
        src_ref=src, dst_ref=dst, send_sem=send, recv_sem=recv, device_id=where, device_id_type=MESH
    )


def step_kernel(
    pattern, sig, tiles, out, wsh, xout, wout, parts, yfar, ysum, ynear, ylast, held, zrecv, msgs, turned, sent, got,
    local_sem, zs, zr, xs_sem, xr, rs, bs, br, ws, wr, ys, yr, qs, qr, cs, cr,
    ps, pr, gs, gr, self_sem, ts, tr, hs, hr
):
    x, zl, zh = lax.axis_index("x"), lax.axis_index("zl"), lax.axis_index("zh")
    y, c = lax.axis_index("y"), lax.axis_index("c")
    right, left = {"x": (x + 1) % NX}, {"x": (x + NX - 1) % NX}
    sibling = {"c": 1 - c}
    place = zh * NZ + zl
    ring = NH * NZ
    up, down = (place + 1) % ring, (place + ring - 1) % ring
    up_id = {"zh": up // NZ, "zl": up % NZ}
    down_id = {"zh": down // NZ, "zl": down % NZ}

    barrier = pltpu.get_barrier_semaphore()
    team = x * NZ + zl
    teams = NX * NZ
    rep = (zh * NY + y) * NC + c
    reps = NH * NY * NC
    source_core = zl // 4

    def rep_id(r):
        return {"zh": r // (NY * NC), "y": (r // NC) % NY, "c": r % NC}

    def team_id(t):
        return {"x": t // NZ, "zl": t % NZ}

    def greet(where):
        pl.semaphore_signal(barrier, inc=1, device_id=where, device_id_type=MESH)

    peers = [{"zl": flip(zl, s)} for s in range(1, NZ)] + [right, left, sibling, up_id, down_id]
    peers += [{"y": (y + d) % NY} for d in range(1, NY)]
    for d in range(1, ring):
        p = (place + d) % ring
        peers.append({"zh": p // NZ, "zl": p % NZ, "c": source_core})
    peers += [rep_id((rep + d) % reps) for d in range(1, reps)]
    for level in range(4):
        peers += [team_id((team + step) % teams) for step in (1 << level, teams - (1 << level))]
    for peer in peers:
        greet(peer)

    @pl.when(source_core != c)
    def _():
        greet(sibling)

    wsh[...] = tiles[0].reshape(wsh.shape).astype(wsh.dtype)
    pl.semaphore_wait(barrier, len(peers) + jnp.where(source_core != c, 1, 0))

    base = c * (NX * NZ)
    mine = base + x * NZ + zl
    own = pltpu.make_async_copy(sig.at[zl], xout.at[mine], local_sem.at[0])
    own.start()
    own_w = pltpu.make_async_copy(wsh, wout.at[c, y, zl, zh], local_sem.at[1])
    own_w.start()
    z_copies = {}

    def z_start(s):
        peer = flip(zl, s)
        copy = remote(sig.at[peer], xout.at[mine], zs.at[s - 1], zr.at[s - 1], {"zl": peer})
        copy.start()
        z_copies[s] = copy

    for s in (4, 1, 2, 3, 5):
        z_start(s)

    def block(dx, s):
        return base + ((x + dx) % NX) * NZ + flip(zl, s)

    def to_sibling(index):
        remote(xout.at[index], xout.at[index], bs, br, sibling).start()

    x_copies = {}

    def spread(s):
        here = xout.at[block(0, s)]
        pair = (
            remote(here, here, xs_sem.at[0, s], xr.at[0, s], right),
            remote(here, here, xs_sem.at[1, s], xr.at[1, s], left),
        )
        for copy in pair:
            copy.start()
        to_sibling(block(0, s))
        x_copies[s] = pair

    relay_copies = {}
    half = xout.shape[1] // 2

    def relay(s):
        pair = []
        for way, (dx, start, where) in enumerate(((NX - 1, 0, right), (1, half, left))):
            x_copies[s][way].wait_recv()
            part = xout.at[block(dx, s), pl.ds(start, half)]
            copy = remote(part, part, rs.at[0, way, s], rs.at[1, way, s], where)
            copy.start()
            to_sibling(block(dx, s))
            pair.append(copy)
        relay_copies[s] = pair

    def finish(s):
        for copy in relay_copies[s]:
            copy.wait_recv()
        to_sibling(block(2, s))

    def origin(e):
        return (place + ring - (e + 1) // 2) % ring if e % 2 else (place + e // 2) % ring

    def shard(e, dy=0):
        o = origin(e)
        return wout.at[c, (y + dy) % NY, o % NZ, o // NZ]

    ring_copies = {}

    def w_ring(t):
        for way, e, steps, where in ((0, max(2 * t - 1, 0), 8, up_id), (1, 2 * t, 7, down_id)):
            if t < steps:
                piece = shard(e)
                copy = remote(wsh if t == 0 else piece, piece, ws.at[way, t], wr.at[way, t], where)
                copy.start()
                ring_copies[way, t] = copy

    forward, backward = {"y": (y + 1) % NY}, {"y": (y + NY - 1) % NY}
    y_copies, y_relays = {}, {}

    def w_forward(e):
        here = shard(e)
        for way, where in enumerate((forward, backward)):
            copy = remote(here, here, ys.at[way, e], yr.at[way, e], where)
            copy.start()
            y_copies[way, e] = copy

    def w_relay(e):
        for way, (dy, start, size, where) in enumerate(((NY - 1, 0, 48, forward), (1, 48, 32, backward))):
            y_copies[way, e].wait_recv()
            part = shard(e, dy).at[pl.ds(start, size)]
            copy = remote(part, part, qs.at[way, e], qr.at[way, e], where)
            copy.start()
            y_relays[way, e] = copy

    def w_pass(t):
        for way in range(2):
            if (way, t) in ring_copies:
                ring_copies[way, t].wait_recv()
        if t < 7:
            w_ring(t + 1)
        for way, e in ((0, 2 * t + 1), (1, 2 * t + 2)):
            if (way, t) in ring_copies:
                w_forward(e)

    def w_relays(t):
        for e in (0,) if t < 0 else (2 * t + 1, 2 * t + 2):
            if (0, e) in y_copies:
                w_relay(e)

    c_copies = []

    def w_sibling(dy):
        part = wout.at[c, (y + dy) % NY, pl.ds(4 * (1 - c), 4)]
        copy = remote(part, part, cs.at[dy], cr.at[dy], sibling)
        copy.start()
        c_copies.append(copy)

    w_ring(0)
    own.wait()
    spread(0)
    own_w.wait()
    w_forward(0)
    for i in range(1, NZ):
        z_copies[i].wait_recv()
        if i + 2 in (6, 7):
            z_start(i + 2)
        spread(i)
        relay(i - 1)
        if i >= 2:
            finish(i - 2)
        w_pass(i - 1)
        w_relays(i - 2)
    relay(NZ - 1)
    w_pass(NZ - 1)
    finish(NZ - 2)
    w_sibling(0)
    w_relays(NZ - 2)
    finish(NZ - 1)
    w_relays(NZ - 1)
    for copy in y_relays.values():
        copy.wait_recv()
    for dy in range(1, NY):
        w_sibling(dy)

    for copy in z_copies.values():
        copy.wait_send()
    for s in range(NZ):
        for copy in x_copies[s]:
            copy.wait_send()
        for copy in relay_copies[s]:
            copy.wait_send()
    for group in (ring_copies, y_copies, y_relays):
        for copy in group.values():
            copy.wait_send()
    for copy in c_copies:
        copy.wait()
    count = NX * NZ
    whole = remote(xout.at[pl.ds(base, count)], xout.at[pl.ds(count - base, count)], bs, br, sibling)
    whole.wait()

    offset = [(pattern[0, k] - team + teams) % teams for k in range(5)]
    y_next, y_last = (y + 1) % NY, (y + NY - 1) % NY
    y_across = (y + 2) % NY

    def y_sends(i):
        j = (zl + i) % 4
        return (
            remote(parts.at[y_across, j, 0], yfar.at[0, j], ps.at[0, i], pr.at[0, i], forward),
            remote(parts.at[y_across, j, 1], yfar.at[1, j], ps.at[1, i], pr.at[1, i], backward),
            remote(parts.at[y_next, j, 1], ynear.at[0, j], ps.at[2, i], pr.at[2, i], forward),
            remote(parts.at[y_last, j, 0], ynear.at[1, j], ps.at[3, i], pr.at[3, i], backward),
        )

    def y_sums(i):
        j = (zl + i) % 4
        return (
            remote(ysum.at[0, j], ylast.at[0, j], ps.at[4, i], pr.at[4, i], forward),
            remote(ysum.at[1, j], ylast.at[1, j], ps.at[5, i], pr.at[5, i], backward),
        )

    def row_products(i, carry):
        j = (zl + i) % 4
        line = x * NZ + 4 * c + j
        columns = [(line + offset[k]) % teams for k in range(5)]
        halves = []
        for part in range(NC):
            total = None
            for k in range(5):
                panel = jnp.concatenate(
                    [
                        wout[cc, yy, 4 * c + j, hh, 16 * k : 16 * k + 16, :]
                        for hh in range(NH)
                        for yy in range(NY)
                        for cc in range(NC)
                    ],
                    axis=0,
                )
                xk = xout[part * teams + columns[k]]
                term = lax.dot_general(panel, xk, (((1,), (1,)), ((), ())), preferred_element_type=jnp.float32)
                total = term if total is None else total + term
            halves.append(total.astype(jnp.bfloat16))
        for k in range(5):
            product = jnp.dot(halves[0], xout[columns[k]], preferred_element_type=jnp.float32)
            product = product + jnp.dot(halves[1], xout[teams + columns[k]], preferred_element_type=jnp.float32)
            product = product.astype(jnp.bfloat16)
            for hh in range(NH):
                for yy in range(NY):
                    start = hh * 128 + yy * 32
                    parts[yy, j, hh, k] = product[start : start + 32, :]
        for copy in y_sends(i):
            copy.start()
        return carry

    lax.fori_loop(0, 4, row_products, 0)

    def final(j, hh, cc):
        return remote(
            held.at[j, hh, cc],
            zrecv.at[place],
            gs.at[j, hh, cc],
            gr.at[place],
            {"zl": 4 * c + j, "zh": hh, "c": cc},
        )

    def is_me(j, hh, cc):
        return (4 * c + j == zl) & (hh == zh) & (cc == c)

    def y_middle(i):
        j = (zl + i) % 4
        sends = y_sends(i)
        for way, near in enumerate((y_next, y_last)):
            sends[way].wait_recv()
            both = parts[near, j, way].astype(jnp.float32) + yfar[way, j].astype(jnp.float32)
            ysum[way, j] = both.astype(jnp.bfloat16)
            y_sums(i)[way].start()

    def y_end(i):
        j = (zl + i) % 4
        sends, sums = y_sends(i), y_sums(i)
        for hh in range(NH):
            sends[3 - hh].wait_recv()
            sums[hh].wait_recv()
            total = parts[y, j, hh].astype(jnp.float32) + ynear[1 - hh, j].astype(jnp.float32)
            total = (total + ylast[hh, j].astype(jnp.float32)).astype(jnp.bfloat16)
            for cc in range(NC):
                held[j, hh, cc] = total[:, 16 * cc : 16 * cc + 16, :]

                @pl.when(is_me(j, hh, cc))
                def _(hh=hh, cc=cc):
                    copy = pltpu.make_async_copy(held.at[j, hh, cc], zrecv.at[place], self_sem)
                    copy.start()
                    copy.wait()

                @pl.when(jnp.logical_not(is_me(j, hh, cc)))
                def _(hh=hh, cc=cc):
                    final(j, hh, cc).start()

    for i in range(4):
        y_middle(i)
        if i:
            y_end(i - 1)
    y_end(3)

    total = None
    for d in range(ring):
        p = (place + d) % ring

        def wait_one(p=p):
            remote(held.at[0, 0, 0], zrecv.at[p], gs.at[0, 0, 0], gr.at[p], sibling).wait_recv()

        if d == 0:
            pl.when(source_core != c)(wait_one)
        else:
            wait_one()
        term = zrecv[p].astype(jnp.float32)
        total = term if total is None else total + term

    slots = total.shape[0]
    lane = lax.broadcasted_iota(jnp.int32, (16, 128), 1) // 16
    for r in range(reps):
        message = jnp.zeros((16, 128), jnp.float32)
        for k in range(slots):
            piece = total[k, :, 128 * (r // 8) : 128 * (r // 8) + 128]
            shift = (16 * k - 16 * (r % 8)) % 128
            if shift:
                piece = pltpu.roll(piece, shift, 1)
            message = jnp.where(lane == k, piece, message)
        msgs[r] = message.astype(msgs.dtype)
    turn_copies = []
    for d in range(1, reps):
        r = (rep + d) % reps
        copy = remote(msgs.at[r], turned.at[rep], ts.at[d - 1], tr.at[d - 1], rep_id(r))
        copy.start()
        turn_copies.append(copy)
    turned[rep] = msgs[rep]
    for copy in turn_copies:
        copy.wait_recv()
    flipped = jnp.transpose(turned[...].astype(jnp.float32).reshape(16 * reps, 128))
    flipped = [flipped[16 * k : 16 * k + 16] for k in range(slots)]

    low = [offset[k] < teams // 2 for k in range(slots)]
    size = [jnp.where(low[k], offset[k], teams - offset[k]) for k in range(slots)]
    first = [size[k] == size[1] for k in range(slots)]

    def pick(values, is_low, is_first):
        chosen = values[slots - 1]
        for k in range(1, slots - 1):
            chosen = jnp.where((low[k] == is_low) & (first[k] == is_first), values[k], chosen)
        return chosen

    sizes = [size[1], pick(size, True, False)]
    ways = []
    for way in range(2):
        ways.append([pick(flipped, way == 1, u == 0) for u in range(2)])
    hops = []
    for level in range(4):
        step = 1 << level
        pair = []
        for way in range(2):
            for u in range(2):
                sent[level, way, u] = ways[way][u].astype(sent.dtype)
            to = (team + (teams - step if way == 0 else step)) % teams
            copy = remote(
                sent.at[level, way], got.at[level, way], hs.at[level, way], hr.at[level, way], team_id(to)
            )
            copy.start()
            pair.append(copy)
        for way in range(2):
            pair[way].wait_recv()
            for u in range(2):
                bit = (sizes[u] // step) % 2 == 1
                ways[way][u] = jnp.where(bit, got[level, way, u].astype(jnp.float32), ways[way][u])
        hops.append(pair)

    length = 32768.0
    column = lax.broadcasted_iota(jnp.int32, (16, 256), 1)
    row = lax.broadcasted_iota(jnp.int32, (16, 256), 0) + rep * 16
    diagonal = column == row
    for k in range(slots):
        tile = tiles[0, k]
        if k == 0:
            back = flipped[0]
        else:
            one = jnp.where(first[k], ways[0][0], ways[0][1])
            two = jnp.where(first[k], ways[1][0], ways[1][1])
            back = jnp.where(low[k], one, two)
        gradient = (total[k] + back) / (2.0 * length)
        if k == 0:
            inverse = 1.0 / jnp.where(diagonal, tile, 1.0)
            gradient = gradient - jnp.where(diagonal, inverse, 0.0)
        value = tile - STEP_SIZE * gradient
        limit = STEP_SIZE * PENALTY
        shrunk = jnp.where(value > limit, value - limit, jnp.where(value < -limit, value + limit, 0.0))
        if k == 0:
            shrunk = jnp.where(diagonal, value, shrunk)
        out[0, k] = shrunk

    for i in range(4):
        j = (zl + i) % 4
        for copy in y_sends(i) + y_sums(i):
            copy.wait_send()
        for hh in range(NH):
            for cc in range(NC):

                @pl.when(jnp.logical_not(is_me(j, hh, cc)))
                def _(j=j, hh=hh, cc=cc):
                    final(j, hh, cc).wait_send()
    for copy in turn_copies:
        copy.wait_send()
    for pair in hops:
        for copy in pair:
            copy.wait_send()


def per_device(signals, omega, pattern):
    rows = signals.shape[0] // NZ
    slots, tile_rows, width = omega.shape[1:]
    dma = pltpu.SemaphoreType.DMA
    bf16, f32 = jnp.bfloat16, jnp.float32
    reps = NH * NY * NC
    ring = NH * NZ
    piece = (slots, 32, width)
    return pl.pallas_call(
        step_kernel,
        out_shape=jax.ShapeDtypeStruct(omega.shape, f32),
        in_specs=[
            pl.BlockSpec(memory_space=pltpu.SMEM),
            pl.BlockSpec(memory_space=pl.ANY),
            pl.BlockSpec(memory_space=pltpu.VMEM),
        ],
        out_specs=pl.BlockSpec(memory_space=pltpu.VMEM),
        scratch_shapes=[
            pltpu.VMEM((slots * tile_rows, width), bf16),
            pltpu.VMEM((NC * NX * NZ, rows, width), bf16),
            pltpu.VMEM((NC, NY, NZ, NH, slots * tile_rows, width), bf16),
            pltpu.VMEM((NY, 4, NH) + piece, bf16),
            pltpu.VMEM((2, 4) + piece, bf16),
            pltpu.VMEM((2, 4) + piece, bf16),
            pltpu.VMEM((2, 4) + piece, bf16),
            pltpu.VMEM((2, 4) + piece, bf16),
            pltpu.VMEM((4, NH, NC, slots, tile_rows, width), bf16),
            pltpu.VMEM((ring, slots, tile_rows, width), bf16),
            pltpu.VMEM((reps, 16, 128), bf16),
            pltpu.VMEM((reps, 16, 128), bf16),
            pltpu.VMEM((4, 2, 2, tile_rows, width), bf16),
            pltpu.VMEM((4, 2, 2, tile_rows, width), bf16),
            dma((2,)),
            dma((NZ - 1,)),
            dma((NZ - 1,)),
            dma((2, NZ)),
            dma((2, NZ)),
            dma((2, 2, NZ)),
            dma,
            dma,
            dma((2, 8)),
            dma((2, 8)),
            dma((2, 16)),
            dma((2, 16)),
            dma((2, 16)),
            dma((2, 16)),
            dma((NY,)),
            dma((NY,)),
            dma((6, 4)),
            dma((6, 4)),
            dma((4, NH, NC)),
            dma((ring,)),
            dma,
            dma((reps - 1,)),
            dma((reps - 1,)),
            dma((4, 2)),
            dma((4, 2)),
        ],
        compiler_params=pltpu.CompilerParams(collective_id=0, has_side_effects=True, vmem_limit_bytes=48 << 20),
        name="step",
    )(pattern, signals.reshape(NZ, rows, width), omega)


def solution(mesh):
    return jax.shard_map(
        per_device,
        mesh=fine_mesh(mesh),
        in_specs=(P(REP, ("x", "zl")), P(("x", "zl"), None, REP, None), P(("x", "zl"), None)),
        out_specs=P(("x", "zl"), None, REP, None),
        check_vma=False,
    )
```

time: 194 us -> 183 us (0.943)
  the two profiles are of different devices: /device:TPU:24 before, /device:TPU:66 now
where the time goes in v4:
time: 183 us; the launch traced here: 182 us
  Pallas kernels  179 us (98%)
  local copies, waits for them, and re-layouts  3.4 us (2%)
    pallas_call x1, Pallas kernels, per_device(): pl.pallas_call(step_kernel, out_shape=jax.ShapeDtypeStruct(omega.shape, f...  179 us

profile of v4, /device:TPU:66, one launch (start us, length us, event | category | flops | bytes accessed | tf_op | source)
XLA Modules:
  0.0 182.5 jit_solution(2016603422890708624)
XLA Ops:
  0.0 0.0 copy-start.2
  0.0 0.7 copy-done.2
  0.7 0.0 copy-start
  0.7 1.2 copy-done
  1.9 0.0 copy-start.1
  1.9 0.9 copy-done.1
  2.8 179.1 %step.1 = f32[1,5,16,256]{3,2,1,0:T(8,128)S(1)} custom-call(s32[1,5]{1,0:T(1,128)S(1)} %copy-done.2, bf16[8,256,256]{2,1,0:T(8,128)(2,1)S(1)} %bitcast.1, f32[1,5,16,256]{3,2,1,0:T(8,128)S(1)} %copy-done.1), custom_call_target="tpu_custom_call" | custom-call | tf_op jit(solution)/shard_map/step/pallas_call | solution.py:461
  181.8 0.6 copy.5
Async XLA Ops:
  0.0 0.7 copy-start.2
  0.7 1.2 copy-start
  1.9 0.9 copy-start.1

commit v5 on v4

--- a/solution.py
+++ b/solution.py
@@ -13,6 +13,10 @@
 NX, NZ, NH, NY, NC = 4, 8, 2, 4, 2
 
 
+W_FIRST = 0
+W_SLOTS = {1: (0,), 2: (1,), 3: (2,), 4: (3,), 5: (4,), 6: (5,), 7: (6,), 9: (7,)}
+
+
 def fine_mesh(mesh):
     return Mesh(mesh.devices.reshape(NX, NZ, NH, NY, NC), ("x", "zl", "zh", "y", "c"))
 
@@ -33,7 +37,7 @@
 
 def step_kernel(
     pattern, sig, tiles, out, wsh, xout, wout, parts, yfar, ysum, ynear, ylast, held, zrecv, msgs, turned, sent, got,
-    local_sem, zs, zr, xs_sem, xr, rs, bs, br, ws, wr, ys, yr, qs, qr, cs, cr,
+    local_sem, zs, zr, xs_sem, xr, rs, bs, br, ws, wr, ys, yr, cs,
     ps, pr, gs, gr, self_sem, ts, tr, hs, hr
 ):
     x, zl, zh = lax.axis_index("x"), lax.axis_index("zl"), lax.axis_index("zh")
@@ -62,29 +66,28 @@
     def greet(where):
         pl.semaphore_signal(barrier, inc=1, device_id=where, device_id_type=MESH)
 
-    peers = [{"zl": flip(zl, s)} for s in range(1, NZ)] + [right, left, sibling, up_id, down_id]
-    peers += [{"y": (y + d) % NY} for d in range(1, NY)]
-    for d in range(1, ring):
-        p = (place + d) % ring
-        peers.append({"zh": p // NZ, "zl": p % NZ, "c": source_core})
-    peers += [rep_id((rep + d) % reps) for d in range(1, reps)]
-    for level in range(4):
-        peers += [team_id((team + step) % teams) for step in (1 << level, teams - (1 << level))]
+    peers = [{"zl": flip(zl, s)} for s in range(1, NZ)] + [right, left, sibling]
+    peers += [{"y": (y + d) % NY, "c": cc} for d in range(1, NY) for cc in range(NC)]
     for peer in peers:
         greet(peer)
 
-    @pl.when(source_core != c)
+    @pl.when(zl == NZ - 1)
     def _():
-        greet(sibling)
-
+        greet(up_id)
+
+    @pl.when(zl == 0)
+    def _():
+        greet(down_id)
+
+    across = jnp.where(zl == NZ - 1, 1, 0) + jnp.where(zl == 0, 1, 0)
     wsh[...] = tiles[0].reshape(wsh.shape).astype(wsh.dtype)
-    pl.semaphore_wait(barrier, len(peers) + jnp.where(source_core != c, 1, 0))
+    pl.semaphore_wait(barrier, len(peers) + across)
 
     base = c * (NX * NZ)
     mine = base + x * NZ + zl
     own = pltpu.make_async_copy(sig.at[zl], xout.at[mine], local_sem.at[0])
     own.start()
-    own_w = pltpu.make_async_copy(wsh, wout.at[c, y, zl, zh], local_sem.at[1])
+    own_w = pltpu.make_async_copy(wsh, wout.at[((c * NY + y) * NZ + zl) * NH + zh], local_sem.at[1])
     own_w.start()
     z_copies = {}
 
@@ -138,37 +141,30 @@
     def origin(e):
         return (place + ring - (e + 1) // 2) % ring if e % 2 else (place + e // 2) % ring
 
-    def shard(e, dy=0):
-        o = origin(e)
-        return wout.at[c, (y + dy) % NY, o % NZ, o // NZ]
+    def shard(o):
+        return wout.at[((c * NY + y) * NZ + o % NZ) * NH + o // NZ]
 
     ring_copies = {}
 
     def w_ring(t):
         for way, e, steps, where in ((0, max(2 * t - 1, 0), 8, up_id), (1, 2 * t, 7, down_id)):
             if t < steps:
-                piece = shard(e)
+                piece = shard(origin(e))
                 copy = remote(wsh if t == 0 else piece, piece, ws.at[way, t], wr.at[way, t], where)
                 copy.start()
                 ring_copies[way, t] = copy
 
     forward, backward = {"y": (y + 1) % NY}, {"y": (y + NY - 1) % NY}
-    y_copies, y_relays = {}, {}
 
     def w_forward(e):
-        here = shard(e)
-        for way, where in enumerate((forward, backward)):
-            copy = remote(here, here, ys.at[way, e], yr.at[way, e], where)
-            copy.start()
-            y_copies[way, e] = copy
-
-    def w_relay(e):
-        for way, (dy, start, size, where) in enumerate(((NY - 1, 0, 48, forward), (1, 48, 32, backward))):
-            y_copies[way, e].wait_recv()
-            part = shard(e, dy).at[pl.ds(start, size)]
-            copy = remote(part, part, qs.at[way, e], qr.at[way, e], where)
-            copy.start()
-            y_relays[way, e] = copy
+        o = origin(e)
+        core = (o % NZ) // 4
+        for d in (1, 3, 2):
+            remote(shard(o), shard(o), ys, yr, {"y": (y + d) % NY, "c": core}).start()
+
+        @pl.when(core != c)
+        def _():
+            remote(shard(o), shard(o), cs, yr, sibling).start()
 
     def w_pass(t):
         for way in range(2):
@@ -180,24 +176,16 @@
             if (way, t) in ring_copies:
                 w_forward(e)
 
-    def w_relays(t):
-        for e in (0,) if t < 0 else (2 * t + 1, 2 * t + 2):
-            if (0, e) in y_copies:
-                w_relay(e)
-
-    c_copies = []
-
-    def w_sibling(dy):
-        part = wout.at[c, (y + dy) % NY, pl.ds(4 * (1 - c), 4)]
-        copy = remote(part, part, cs.at[dy], cr.at[dy], sibling)
-        copy.start()
-        c_copies.append(copy)
-
-    w_ring(0)
+    def w_passes(steps):
+        for t in steps:
+            w_pass(t)
+
     own.wait()
     spread(0)
     own_w.wait()
-    w_forward(0)
+    if W_FIRST == 0:
+        w_ring(0)
+        w_forward(0)
     for i in range(1, NZ):
         z_copies[i].wait_recv()
         if i + 2 in (6, 7):
@@ -206,20 +194,17 @@
         relay(i - 1)
         if i >= 2:
             finish(i - 2)
-        w_pass(i - 1)
-        w_relays(i - 2)
+        if i == W_FIRST:
+            w_ring(0)
+            w_forward(0)
+        w_passes(W_SLOTS.get(i, ()))
+    w_passes(W_SLOTS.get(8, ()))
     relay(NZ - 1)
-    w_pass(NZ - 1)
+    w_passes(W_SLOTS.get(9, ()))
     finish(NZ - 2)
-    w_sibling(0)
-    w_relays(NZ - 2)
+    w_passes(W_SLOTS.get(10, ()))
     finish(NZ - 1)
-    w_relays(NZ - 1)
-    for copy in y_relays.values():
-        copy.wait_recv()
-    for dy in range(1, NY):
-        w_sibling(dy)
-
+    w_passes(W_SLOTS.get(11, ()))
     for copy in z_copies.values():
         copy.wait_send()
     for s in range(NZ):
@@ -227,11 +212,15 @@
             copy.wait_send()
         for copy in relay_copies[s]:
             copy.wait_send()
-    for group in (ring_copies, y_copies, y_relays):
-        for copy in group.values():
-            copy.wait_send()
-    for copy in c_copies:
-        copy.wait()
+    for copy in ring_copies.values():
+        copy.wait_send()
+
+    def shards(count):
+        return wout.at[pl.ds(0, count)]
+
+    remote(shards(3 * ring), shards(3 * ring), ys, yr, sibling).wait_send()
+    remote(shards(ring // 2), shards(ring // 2), cs, yr, sibling).wait_send()
+    remote(shards(7 * ring // 2), shards(7 * ring // 2), ys, yr, sibling).wait_recv()
     count = NX * NZ
     whole = remote(xout.at[pl.ds(base, count)], xout.at[pl.ds(count - base, count)], bs, br, sibling)
     whole.wait()
@@ -266,7 +255,7 @@
             for k in range(5):
                 panel = jnp.concatenate(
                     [
-                        wout[cc, yy, 4 * c + j, hh, 16 * k : 16 * k + 16, :]
+                        wout[((cc * NY + yy) * NZ + 4 * c + j) * NH + hh, 16 * k : 16 * k + 16, :]
                         for hh in range(NH)
                         for yy in range(NY)
                         for cc in range(NC)
@@ -470,7 +459,7 @@
         scratch_shapes=[
             pltpu.VMEM((slots * tile_rows, width), bf16),
             pltpu.VMEM((NC * NX * NZ, rows, width), bf16),
-            pltpu.VMEM((NC, NY, NZ, NH, slots * tile_rows, width), bf16),
+            pltpu.VMEM((NC * NY * NZ * NH, slots * tile_rows, width), bf16),
             pltpu.VMEM((NY, 4, NH) + piece, bf16),
             pltpu.VMEM((2, 4) + piece, bf16),
             pltpu.VMEM((2, 4) + piece, bf16),
@@ -492,12 +481,9 @@
             dma,
             dma((2, 8)),
             dma((2, 8)),
-            dma((2, 16)),
-            dma((2, 16)),
-            dma((2, 16)),
-            dma((2, 16)),
-            dma((NY,)),
-            dma((NY,)),
+            dma,
+            dma,
+            dma,
             dma((6, 4)),
             dma((6, 4)),
             dma((4, NH, NC)),

time: 183 us -> 172 us (0.940)
  Pallas kernels: 179 us -> 168 us
    pallas_call x1, Pallas kernels: 179 us -> 168 us  [per_device(): pl.pallas_call(step_kernel, out_shape=jax.ShapeDtypeStruct(omega.shape, f...]
where the time goes in v5:
time: 172 us; the launch traced here: 171 us
  Pallas kernels  168 us (98%)
  local copies, waits for them, and re-layouts  3.4 us (2%)
    pallas_call x1, Pallas kernels, per_device(): pl.pallas_call(step_kernel, out_shape=jax.ShapeDtypeStruct(omega.shape, f...  168 us

profile of v5, /device:TPU:66, one launch (start us, length us, event | category | flops | bytes accessed | tf_op | source)
XLA Modules:
  0.0 171.5 jit_solution(5846491359387545025)
XLA Ops:
  0.0 0.0 copy-start.2
  0.0 0.7 copy-done.2
  0.7 0.0 copy-start
  0.7 1.2 copy-done
  1.9 0.0 copy-start.1
  1.9 0.9 copy-done.1
  2.8 168.1 %step.1 = f32[1,5,16,256]{3,2,1,0:T(8,128)S(1)} custom-call(s32[1,5]{1,0:T(1,128)S(1)} %copy-done.2, bf16[8,256,256]{2,1,0:T(8,128)(2,1)S(1)} %bitcast.1, f32[1,5,16,256]{3,2,1,0:T(8,128)S(1)} %copy-done.1), custom_call_target="tpu_custom_call" | custom-call | tf_op jit(solution)/shard_map/step/pallas_call | solution.py:450
  170.8 0.6 copy.5
Async XLA Ops:
  0.0 0.7 copy-start.2
  0.7 1.2 copy-start
  1.9 0.9 copy-start.1

commit v6 on v5

--- a/solution.py
+++ b/solution.py
@@ -13,6 +13,8 @@
 NX, NZ, NH, NY, NC = 4, 8, 2, 4, 2
 
 
+Y_AHEAD = 1
+Y_LAG = 0
 W_FIRST = 0
 W_SLOTS = {1: (0,), 2: (1,), 3: (2,), 4: (3,), 5: (4,), 6: (5,), 7: (6,), 9: (7,)}
 
@@ -274,8 +276,12 @@
                 for yy in range(NY):
                     start = hh * 128 + yy * 32
                     parts[yy, j, hh, k] = product[start : start + 32, :]
-        for copy in y_sends(i):
-            copy.start()
+
+        @pl.when(i < Y_AHEAD)
+        def _():
+            for copy in y_sends(i):
+                copy.start()
+
         return carry
 
     lax.fori_loop(0, 4, row_products, 0)
@@ -300,6 +306,9 @@
             both = parts[near, j, way].astype(jnp.float32) + yfar[way, j].astype(jnp.float32)
             ysum[way, j] = both.astype(jnp.bfloat16)
             y_sums(i)[way].start()
+        if i + Y_AHEAD < 4:
+            for copy in y_sends(i + Y_AHEAD):
+                copy.start()
 
     def y_end(i):
         j = (zl + i) % 4
@@ -324,9 +333,10 @@
 
     for i in range(4):
         y_middle(i)
-        if i:
-            y_end(i - 1)
-    y_end(3)
+        if i >= Y_LAG:
+            y_end(i - Y_LAG)
+    for i in range(4 - Y_LAG, 4):
+        y_end(i)
 
     total = None
     for d in range(ring):

time: 172 us -> 161 us (0.936)
  the two profiles are of different devices: /device:TPU:66 before, /device:TPU:90 now
where the time goes in v6:
time: 161 us
  Pallas kernels  157 us (98%)
  local copies, waits for them, and re-layouts  3.4 us (2%)
    pallas_call x1, Pallas kernels, per_device(): pl.pallas_call(step_kernel, out_shape=jax.ShapeDtypeStruct(omega.shape, f...  157 us
    unnamed x7, local copies, waits for them, and re-layouts  3.4 us

profile of v6, /device:TPU:90, one launch (start us, length us, event | category | flops | bytes accessed | tf_op | source)
XLA Modules:
  0.0 160.6 jit_solution(10834465141994750032)
XLA Ops:
  0.0 0.0 copy-start.2
  0.0 0.7 copy-done.2
  0.7 0.0 copy-start
  0.7 1.2 copy-done
  1.9 0.0 copy-start.1
  1.9 0.9 copy-done.1
  2.8 157.2 %step.1 = f32[1,5,16,256]{3,2,1,0:T(8,128)S(1)} custom-call(s32[1,5]{1,0:T(1,128)S(1)} %copy-done.2, bf16[8,256,256]{2,1,0:T(8,128)(2,1)S(1)} %bitcast.1, f32[1,5,16,256]{3,2,1,0:T(8,128)S(1)} %copy-done.1), custom_call_target="tpu_custom_call" | custom-call | tf_op jit(solution)/shard_map/step/pallas_call | solution.py:460
  160.0 0.6 copy.5
Async XLA Ops:
  0.0 0.7 copy-start.2
  0.7 1.2 copy-start
  1.9 0.9 copy-start.1

commit v7 on v6

--- a/solution.py
+++ b/solution.py
@@ -364,7 +364,7 @@
             message = jnp.where(lane == k, piece, message)
         msgs[r] = message.astype(msgs.dtype)
     turn_copies = []
-    for d in range(1, reps):
+    for d in (8, 9, 7, 10, 6, 11, 5, 12, 4, 13, 3, 14, 2, 15, 1):
         r = (rep + d) % reps
         copy = remote(msgs.at[r], turned.at[rep], ts.at[d - 1], tr.at[d - 1], rep_id(r))
         copy.start()
@@ -390,23 +390,25 @@
     for way in range(2):
         ways.append([pick(flipped, way == 1, u == 0) for u in range(2)])
     hops = []
-    for level in range(4):
+    for level in range(5):
         step = 1 << level
         pair = []
         for way in range(2):
-            for u in range(2):
-                sent[level, way, u] = ways[way][u].astype(sent.dtype)
-            to = (team + (teams - step if way == 0 else step)) % teams
-            copy = remote(
-                sent.at[level, way], got.at[level, way], hs.at[level, way], hr.at[level, way], team_id(to)
-            )
-            copy.start()
-            pair.append(copy)
-        for way in range(2):
-            pair[way].wait_recv()
-            for u in range(2):
-                bit = (sizes[u] // step) % 2 == 1
-                ways[way][u] = jnp.where(bit, got[level, way, u].astype(jnp.float32), ways[way][u])
+            if level:
+                hops[level - 1][way].wait_recv()
+                for u in range(2):
+                    bit = (sizes[u] // (step // 2)) % 2 == 1
+                    arrived = got[level - 1, way, u].astype(jnp.float32)
+                    ways[way][u] = jnp.where(bit, arrived, ways[way][u])
+            if level < 4:
+                for u in range(2):
+                    sent[level, way, u] = ways[way][u].astype(sent.dtype)
+                to = (team + (teams - step if way == 0 else step)) % teams
+                copy = remote(
+                    sent.at[level, way], got.at[level, way], hs.at[level, way], hr.at[level, way], team_id(to)
+                )
+                copy.start()
+                pair.append(copy)
         hops.append(pair)
 
     length = 32768.0

time: 161 us -> 161 us (level)
  the two profiles are of different devices: /device:TPU:90 before, /device:TPU:34 now
where the time goes in v7:
time: 161 us; the launch traced here: 160 us
  Pallas kernels  157 us (98%)
  local copies, waits for them, and re-layouts  3.4 us (2%)
    pallas_call x1, Pallas kernels, per_device(): pl.pallas_call(step_kernel, out_shape=jax.ShapeDtypeStruct(omega.shape, f...  157 us
    unnamed x7, local copies, waits for them, and re-layouts  3.4 us

profile of v7, /device:TPU:34, one launch (start us, length us, event | category | flops | bytes accessed | tf_op | source)
XLA Modules:
  0.0 160.3 jit_solution(5502669705485117251)
XLA Ops:
  0.0 0.0 copy-start.2
  0.0 0.7 copy-done.2
  0.7 0.0 copy-start
  0.7 1.2 copy-done
  1.9 0.0 copy-start.1
  1.9 0.9 copy-done.1
  2.8 156.9 %step.1 = f32[1,5,16,256]{3,2,1,0:T(8,128)S(1)} custom-call(s32[1,5]{1,0:T(1,128)S(1)} %copy-done.2, bf16[8,256,256]{2,1,0:T(8,128)(2,1)S(1)} %bitcast.1, f32[1,5,16,256]{3,2,1,0:T(8,128)S(1)} %copy-done.1), custom_call_target="tpu_custom_call" | custom-call | tf_op jit(solution)/shard_map/step/pallas_call | solution.py:462
  159.7 0.6 copy.5
Async XLA Ops:
  0.0 0.7 copy-start.2
  0.7 1.2 copy-start
  1.9 0.9 copy-start.1
